TPU v7x, 32 devices: a whole 2x2x4 slice. The times are simulated.
32 devices in a mesh: dp: 4 (over y, core), pipe: 2 (over x), expert: 4 (over z).
Axes of the slice: x: 2, y: 2, z: 4, core: 2. Of those that a mesh axis runs over, the one named last changes fastest.
Arguments:
- activations: bfloat16 [2, 2048, 2048], P('pipe', ('dp', 'expert')), may hold values from -6 to 6
- out_grad: bfloat16 [2, 2048, 2048], P('pipe', ('dp', 'expert')), may hold values from -6 to 6
- slot_token: int32 [2, 16, 4, 4], P('pipe', ('dp', 'expert')), may hold values from 0 to 127, as said below
- slot_count: int32 [2, 16, 4], P('pipe', ('dp', 'expert')), may hold values from 0 to 4, as said below
- gate_prob: bfloat16 [2, 16, 4, 4], P('pipe', ('dp', 'expert')), may hold values from 0.049804688 to 1
- w_up: bfloat16 [2, 4, 2048, 768], P('pipe', 'expert'), may hold values from -0.125 to 0.125
- w_down: bfloat16 [2, 4, 768, 2048], P('pipe', 'expert'), may hold values from -0.21875 to 0.21875
Outputs:
- grad_prev: bfloat16 [2, 2048, 2048], P('pipe', ('dp', 'expert'))
- grad_gate: bfloat16 [2, 16, 4, 4], P('pipe', ('dp', 'expert'))
- grad_up: bfloat16 [2, 4, 2048, 768], P('pipe', 'expert', 'dp')
- grad_down: bfloat16 [2, 4, 768, 2048], P('pipe', 'expert', None, 'dp')
Inputs may be any that keep to these rules, and one draw needn't show every extreme that they name: `slot_token`: the 4 slots of one source device and one expert name distinct tokens of that device. `slot_count`: in each section some expert gets 4 used slots from every source device; slots at or past the count are unused.
All inputs are finite; a program needn't handle non-finite values.
Results may differ from a plain program's by a relative error of at most 0.009.
Values may be sent and summed in bfloat16 or wider, within the bound.
No kernel may reach another device: no remote copies, remote signals or barrier semaphores. Data moves between devices by JAX's collectives and lax.ppermute only.
A program may use at most 64 MiB of HBM per device.

v0:
```python
import functools
import itertools

import jax
import jax.numpy as jnp
from jax import lax
from jax.experimental import pallas as pl
from jax.experimental.pallas import tpu as pltpu
from jax.sharding import PartitionSpec as P


BF16 = jnp.bfloat16
F32 = jnp.float32
LANES = 128
PERMUTE_LIMIT = 4
KERNEL_VMEM = 24 << 20


def row_marks(rows, width, capacity):
    row = lax.broadcasted_iota(jnp.int32, (rows, width), 0)
    inside = row & (2 * capacity - 1)
    group = lax.shift_right_logical(row, (2 * capacity).bit_length() - 1)
    return group, inside & (capacity - 1), inside < capacity


def stacked_rows(blocks, start, stop):
    return jnp.concatenate([block[:, start:stop].astype(F32) for block in blocks], axis=0)


def blocks_of(refs):
    if len(refs) == 1 and len(refs[0].shape) == 3:
        return [refs[0].at[k] for k in range(refs[0].shape[0])]
    return list(refs)


def own_place(axis, size):
    return lax.axis_index(axis) if size <= PERMUTE_LIMIT else 0


def pack_kernel(acts_far, grads_far, ids_far, counts_far, probs_far, *refs):
    outs, acts, grads, ids, counts, probs, sems = refs[:-6], *refs[-6:]
    near = (ids, counts, probs, acts, grads)
    far = (ids_far, counts_far, probs_far, acts_far, grads_far)
    copies = [pltpu.make_async_copy(a, b, sems.at[k]) for k, (a, b) in enumerate(zip(far, near))]
    for copy in copies:
        copy.start()
    for copy in copies[:3]:
        copy.wait()
    tokens, width = acts.shape[1:]
    experts, capacity = ids.shape[2:]
    rows = 2 * experts * capacity
    place = own_place("expert", experts)
    group, slot, _ = row_marks(rows, capacity, capacity)
    dest = group ^ place
    id_rows = ids[0, 0].astype(F32)
    prob_rows = probs[0, 0].astype(F32)
    id_grid = jnp.zeros((rows, capacity), F32)
    prob_grid = jnp.zeros((rows, capacity), F32)
    for e in range(experts):
        here = dest == e
        id_grid = jnp.where(here, id_rows[e : e + 1], id_grid)
        prob_grid = jnp.where(here, prob_rows[e : e + 1], prob_grid)
    at_slot = lax.broadcasted_iota(jnp.int32, (rows, capacity), 1) == slot
    id_col = jnp.sum(jnp.where(at_slot, id_grid, 0.0), axis=1, keepdims=True)
    prob_col = jnp.sum(jnp.where(at_slot, prob_grid, 0.0), axis=1, keepdims=True)
    dest_wide = row_marks(rows, experts, capacity)[0] ^ place
    at_dest = lax.broadcasted_iota(jnp.int32, (rows, experts), 1) == dest_wide
    count_row = counts[0].astype(F32)
    count_col = jnp.sum(jnp.where(at_dest, count_row, 0.0), axis=1, keepdims=True)
    live = slot[:, :1].astype(F32) < count_col
    prob_col = jnp.where(live, prob_col, 0.0)
    _, _, first_wide = row_marks(rows, tokens, capacity)
    lane = lax.broadcasted_iota(jnp.int32, (rows, tokens), 1).astype(F32)
    hit = jnp.where(lane == id_col, 1.0, 0.0)
    hit_live = jnp.where(live, hit, 0.0)
    pick_act = jnp.where(first_wide, hit, 0.0).astype(BF16)
    pick_grad = jnp.where(first_wide, 0.0, hit_live).astype(BF16)
    for copy in copies[3:]:
        copy.wait()
    picked = jnp.dot(pick_act, acts[0], preferred_element_type=F32)
    picked = picked + jnp.dot(pick_grad, grads[0], preferred_element_type=F32)
    tail_lane = lax.broadcasted_iota(jnp.int32, (rows, LANES), 1)
    tail = jnp.where(tail_lane == 0, prob_col, jnp.where(tail_lane == 1, id_col, 0.0))
    size = 2 * capacity
    for k, out in enumerate(blocks_of(outs)):
        out[:, :width] = picked[k * size : (k + 1) * size].astype(BF16)
        out[:, width:] = tail[k * size : (k + 1) * size].astype(BF16)


def load_kernel(up_far, down_far, _, up, down, sems):
    copies = [
        pltpu.make_async_copy(up_far, up, sems.at[0]),
        pltpu.make_async_copy(down_far, down, sems.at[1]),
    ]
    for copy in copies:
        copy.start()
    for copy in copies:
        copy.wait()


def expert_kernel(capacity, replicas, n_blocks, *refs):
    blocks = blocks_of(refs[:n_blocks])
    up, down = refs[n_blocks : n_blocks + 2]
    outs = blocks_of(refs[n_blocks + 2 : -2])
    gate_out, scaled = refs[-2:]
    width, hidden_width = up.shape[2:]
    rows = 2 * capacity * len(blocks)
    part = width // replicas
    packed = stacked_rows(blocks, 0, width)
    tail = stacked_rows(blocks, width, width + LANES)
    prob = tail[:, 0:1]
    packed_bf16 = packed.astype(BF16)
    pre_act = jnp.dot(packed_bf16, up[0, 0], preferred_element_type=F32)
    grad_proj = lax.dot_general(
        packed_bf16, down[0, 0], (((1,), (1,)), ((), ())), preferred_element_type=F32
    )
    grad_proj = pltpu.roll(grad_proj, rows - capacity, 0)
    _, _, first_wide = row_marks(rows, width, capacity)
    scaled[...] = jnp.where(first_wide, packed, prob * packed).astype(BF16)
    logistic = jax.nn.sigmoid(pre_act)
    hidden = (pre_act * logistic).astype(BF16).astype(F32)
    slope = logistic * (1.0 + pre_act * (1.0 - logistic))
    act_grad = prob * grad_proj * slope
    gate = jnp.sum(hidden * grad_proj, axis=1, keepdims=True)
    lane = lax.broadcasted_iota(jnp.int32, (rows, LANES), 1)
    gate_out[...] = jnp.where(lane == 0, gate, tail).astype(BF16)
    _, _, first = row_marks(rows, hidden_width, capacity)
    both = jnp.where(first, act_grad, pltpu.roll(hidden, capacity, 0)).astype(BF16)
    place = own_place("dp", replicas)
    for k, out in enumerate(outs):
        column = pl.multiple_of((place ^ k) * part, LANES)
        out[:, :hidden_width] = both
        out[:, hidden_width:] = scaled[:, pl.ds(column, part)]


def back_kernel(capacity, own, up, gate_own, gate_other, *outs):
    width, hidden_width = up.shape[2:]
    rows = own.shape[0]
    half = width // 2
    row_grad = lax.dot_general(
        own[:, :hidden_width], up[0, 0], (((1,), (1,)), ((), ())), preferred_element_type=F32
    )
    _, _, first = row_marks(rows, half, capacity)
    body = jnp.where(first, row_grad[:, :half], pltpu.roll(row_grad[:, half:], capacity, 0))
    lane = lax.broadcasted_iota(jnp.int32, (rows, LANES), 1)
    tail = jnp.where(lane == 0, gate_other[...].astype(F32), gate_own[...].astype(F32))
    size = 2 * capacity
    for k, out in enumerate(blocks_of(outs)):
        out[:, :half] = body[k * size : (k + 1) * size].astype(BF16)
        out[:, half:] = tail[k * size : (k + 1) * size].astype(BF16)


def weight_kernel(capacity, n_blocks, *refs):
    blocks = blocks_of(refs[:n_blocks])
    grad_up, grad_down = refs[n_blocks:]
    hidden_width = grad_up.shape[3]
    joined = jnp.concatenate([block[...] for block in blocks], axis=0)
    both, sides = joined[:, :hidden_width], joined[:, hidden_width:]
    _, _, first = row_marks(both.shape[0], both.shape[1], capacity)
    act_grad = jnp.where(first, both, jnp.zeros_like(both))
    grad_up[0, 0] = lax.dot_general(
        sides, act_grad, (((0,), (0,)), ((), ())), preferred_element_type=F32
    ).astype(BF16)
    _, _, first = row_marks(sides.shape[0], sides.shape[1], capacity)
    scaled = jnp.where(first, jnp.zeros_like(sides), sides)
    grad_down[0, 0] = lax.dot_general(
        both, scaled, (((0,), (0,)), ((), ())), preferred_element_type=F32
    ).astype(BF16)


def combine_kernel(capacity, sections, n_blocks, *refs):
    blocks = blocks_of(refs[:n_blocks])
    grad_prev, grad_gate = refs[n_blocks:]
    tokens, width = grad_prev.shape[1:]
    experts = len(blocks)
    half = width // 2
    rows = 2 * capacity * experts
    body = stacked_rows(blocks, 0, half).astype(BF16)
    tail = stacked_rows(blocks, half, half + LANES)
    _, _, first = row_marks(rows, tokens, capacity)
    lane = lax.broadcasted_iota(jnp.int32, (rows, tokens), 1).astype(F32)
    kept = jnp.where(lax.axis_index("pipe") == sections - 1, 0.0, 1.0)
    hit = jnp.where(lane == tail[:, 1:2], kept, 0.0)
    for part, mark in enumerate((first, jnp.logical_not(first))):
        one_hot = jnp.where(mark, hit, 0.0).astype(BF16)
        grad_prev[0, :, part * half : (part + 1) * half] = lax.dot_general(
            one_hot, body, (((0,), (0,)), ((), ())), preferred_element_type=F32
        ).astype(BF16)
    _, slot, first = row_marks(rows, capacity, capacity)
    at_slot = lax.broadcasted_iota(jnp.int32, (rows, capacity), 1) == slot
    gates = jnp.where(jnp.logical_and(at_slot, first), tail[:, 0:1], 0.0).astype(BF16)
    column = lax.broadcasted_iota(jnp.int32, (experts, rows), 1)
    source = lax.shift_right_logical(column, (2 * capacity).bit_length() - 1)
    source = source ^ own_place("expert", experts)
    wanted = source == lax.broadcasted_iota(jnp.int32, (experts, rows), 0)
    grad_gate[0, 0] = jnp.dot(
        jnp.where(wanted, 1.0, 0.0).astype(BF16), gates, preferred_element_type=F32
    ).astype(BF16)


def call(kernel, out_shape, args, flops, n_bytes, scratch=(), far=(), near_out=True):
    near_spec = pl.BlockSpec(memory_space=pltpu.VMEM)
    far_spec = pl.BlockSpec(memory_space=pl.ANY)
    args = [
        pltpu.with_memory_space_constraint(a, pltpu.HBM if k in far else pltpu.VMEM)
        for k, a in enumerate(args)
    ]
    if near_out:
        out_shape = [pltpu.VMEM(s.shape, s.dtype) for s in out_shape]
    return pl.pallas_call(
        kernel,
        out_shape=out_shape,
        in_specs=[far_spec if k in far else near_spec for k in range(len(args))],
        out_specs=[near_spec] * len(out_shape),
        scratch_shapes=list(scratch),
        compiler_params=pltpu.CompilerParams(vmem_limit_bytes=KERNEL_VMEM),
        cost_estimate=pl.CostEstimate(flops=flops, bytes_accessed=n_bytes, transcendentals=0),
    )(*args)


def permuted(block, axes, route):
    sizes = [lax.axis_size(axis) for axis in axes]

    def flat(place):
        return functools.reduce(lambda total, pair: total * pair[1] + pair[0], zip(place, sizes), 0)

    places = list(itertools.product(*[range(size) for size in sizes]))
    pairs = [(flat(place), flat(route(place))) for place in places]
    return lax.ppermute(block, axes if len(axes) > 1 else axes[0], pairs)


def message_shapes(count, rows, width):
    if count <= PERMUTE_LIMIT:
        return [jax.ShapeDtypeStruct((rows, width), BF16)] * count
    return [jax.ShapeDtypeStruct((count, rows, width), BF16)]


def exchanged(blocks, axis):
    if len(blocks) == 1:
        return [lax.all_to_all(blocks[0], axis, split_axis=0, concat_axis=0, tiled=True)]
    sent = [
        permuted(b, (axis,), lambda p, k=k: (p[0] ^ k,))
        for k, b in enumerate(blocks)
        if k
    ]
    return [blocks[0]] + sent


def sent_back(blocks, sections):
    if len(blocks) == 1:
        moved = permuted(blocks[0], ("pipe",), lambda p: ((p[0] - 1) % sections,))
        return [lax.all_to_all(moved, "expert", split_axis=0, concat_axis=0, tiled=True)]
    return [
        permuted(b, ("pipe", "expert"), lambda p, k=k: ((p[0] - 1) % sections, p[1] ^ k))
        for k, b in enumerate(blocks)
    ]


def per_device(activations, out_grad, slot_token, slot_count, gate_prob, w_up, w_down):
    tokens, width = activations.shape[1:]
    experts, capacity = slot_token.shape[2:]
    hidden_width = w_up.shape[3]
    replicas = lax.axis_size("dp")
    sections = lax.axis_size("pipe")
    size = 2 * capacity
    rows = size * experts
    part = width // replicas
    half = width // 2
    sources = (activations, out_grad, slot_token, slot_count, gate_prob)
    packed = call(
        pack_kernel,
        message_shapes(experts, size, width + LANES),
        sources,
        4 * rows * tokens * width,
        4 * tokens * width,
        [pltpu.VMEM(a.shape, a.dtype) for a in sources] + [pltpu.SemaphoreType.DMA((5,))],
        far=range(5),
    )
    near_up, near_down = call(
        load_kernel,
        [jax.ShapeDtypeStruct(w.shape, w.dtype) for w in (w_up, w_down)],
        (w_up, w_down, packed[0]),
        0,
        4 * width * hidden_width,
        [pltpu.SemaphoreType.DMA((2,))],
        far=range(2),
    )
    held = exchanged(packed, "expert")
    made = call(
        functools.partial(expert_kernel, capacity, replicas, len(held)),
        message_shapes(replicas, rows, hidden_width + part)
        + [jax.ShapeDtypeStruct((rows, LANES), BF16)],
        (*held, near_up, near_down),
        4 * rows * width * hidden_width,
        4 * width * hidden_width,
        [pltpu.VMEM((rows, width), BF16)],
    )
    shares, gate_own = made[:-1], made[-1]
    gate_other = permuted(gate_own, ("pipe",), lambda p: ((p[0] + 1) % sections,))
    joined = exchanged(shares, "dp")
    own = shares[0] if len(shares) > 1 else shares[0][0]
    back = call(
        functools.partial(back_kernel, capacity),
        message_shapes(experts, size, half + LANES),
        (own, near_up, gate_own, gate_other),
        2 * rows * width * hidden_width,
        2 * width * hidden_width,
    )
    returned = sent_back(back, sections)
    grad_up, grad_down = call(
        functools.partial(weight_kernel, capacity, len(joined)),
        [
            jax.ShapeDtypeStruct((1, 1, part, hidden_width), BF16),
            jax.ShapeDtypeStruct((1, 1, hidden_width, part), BF16),
        ],
        tuple(joined),
        4 * replicas * rows * part * hidden_width,
        4 * part * hidden_width,
        near_out=False,
    )
    grad_prev, grad_gate = call(
        functools.partial(combine_kernel, capacity, sections, len(returned)),
        [
            jax.ShapeDtypeStruct((1, tokens, width), BF16),
            jax.ShapeDtypeStruct((1, 1, experts, capacity), BF16),
        ],
        tuple(returned),
        2 * rows * tokens * width,
        2 * tokens * width,
        near_out=False,
    )
    return grad_prev, grad_gate, grad_up, grad_down


def solution(mesh):
    by_token = ("dp", "expert")
    placed = (
        P("pipe", by_token, None),
        P("pipe", by_token, None),
        P("pipe", by_token, None, None),
        P("pipe", by_token, None),
        P("pipe", by_token, None, None),
        P("pipe", "expert", None, None),
        P("pipe", "expert", None, None),
    )
    return jax.shard_map(
        per_device,
        mesh=mesh,
        in_specs=placed,
        out_specs=(
            P("pipe", by_token, None),
            P("pipe", by_token, None, None),
            P("pipe", "expert", "dp", None),
            P("pipe", "expert", None, "dp"),
        ),
        check_vma=False,
    )
```

profile of v0, /device:TPU:0, one launch (start us, length us, event | category | flops | bytes accessed | tf_op | source)
XLA Modules:
  0.0 37.3 jit_solution(4549972157814384713)
XLA Ops:
  0.6 1.6 %shard_map.102 = (bf16[8,2176]{1,0:T(8,128)(2,1)S(1)}, bf16[8,2176]{1,0:T(8,128)(2,1)S(1)}, bf16[8,2176]{1,0:T(8,128)(2,1)S(1)}, bf16[8,2176]{1,0:T(8,128)(2,1)S(1)}) custom-call(bf16[1,128,2048]{2,1,0:T(8,128)(2,1)} %acts_far.1, bf16[1,128,2048]{2,1,0:T(8,128)(2,1)} %grads_far.1, s32[1,1,4,4]{3,2,1,0:T(4,128)} %ids_far.1, s32[1,1,4]{2,1,0:T(1,128)} %counts_far.1, ...), custom_call_target="tpu_custom_call" | custom-call | flops 33554432 | bytes 1048576 | tf_op jit(solution)/shard_map/pallas_call | solution.py:210
  2.2 3.1 %collective-permute-start = (bf16[8,2176]{1,0:T(8,128)(2,1)S(1)}, bf16[8,2176]{1,0:T(8,128)(2,1)S(1)}, u32[]{:S(2)}, u32[]{:S(2)}) collective-permute-start(bf16[8,2176]{1,0:T(8,128)(2,1)S(1)} %get-tuple-element.24), channel_id=1, source_target_pairs={{0,1},{1,0},{2,3},{3,2},{4,5},{5,4},{6,7},{7,6},{8,9},{9,8},{10,11... | collective-permute-start | bytes 104456 | tf_op jit(solution)/shard_map/ppermute | solution.py:229
  5.3 2.6 %collective-permute-start.1 = (bf16[8,2176]{1,0:T(8,128)(2,1)S(1)}, bf16[8,2176]{1,0:T(8,128)(2,1)S(1)}, u32[]{:S(2)}, u32[]{:S(2)}) collective-permute-start(bf16[8,2176]{1,0:T(8,128)(2,1)S(1)} %get-tuple-element.25), channel_id=1, source_target_pairs={{0,2},{1,3},{2,0},{3,1},{4,6},{5,7},{6,4},{7,5},{8,10},{9,11},{10,... | collective-permute-start | bytes 104456 | tf_op jit(solution)/shard_map/ppermute | solution.py:229
  7.9 0.0 collective-permute-start.2
  7.9 2.9 %shard_map.103 = (bf16[1,1,2048,768]{3,2,1,0:T(8,128)(2,1)S(1)}, bf16[1,1,768,2048]{3,2,1,0:T(8,128)(2,1)S(1)}) custom-call(bf16[1,1,2048,768]{3,2,1,0:T(8,128)(2,1)} %up_far.1, bf16[1,1,768,2048]{3,2,1,0:T(8,128)(2,1)} %down_far.1, bf16[8,2176]{1,0:T(8,128)(2,1)S(1)} %get-tuple-element.23._.refs_0_), custom_call_target="tpu_custom_call" | custom-call | bytes 6291456 | tf_op jit(solution)/shard_map/pallas_call | solution.py:210
  10.8 0.0 collective-permute-done.refs_1_
  10.8 0.0 collective-permute-done.1.refs_2_
  10.8 2.8 %collective-permute-done.2.refs_3_ = bf16[8,2176]{1,0:T(8,128)(2,1)S(1)} collective-permute-done((bf16[8,2176]{1,0:T(8,128)(2,1)S(1)}, bf16[8,2176]{1,0:T(8,128)(2,1)S(1)}, u32[]{:S(2)}, u32[]{:S(2)}) %collective-permute-start.2) | collective-permute-done | bytes 34848 | tf_op jit(solution)/shard_map/ppermute | solution.py:229
  13.6 1.6 %shard_map.104 = (bf16[32,1280]{1,0:T(8,128)(2,1)S(1)}, bf16[32,1280]{1,0:T(8,128)(2,1)S(1)}, bf16[32,1280]{1,0:T(8,128)(2,1)S(1)}, bf16[32,1280]{1,0:T(8,128)(2,1)S(1)}, bf16[32,128]{1,0:T(8,128)(2,1)S(1)}) custom-call(bf16[8,2176]{1,0:T(8,128)(2,1)S(1)} %get-tuple-element.23._.refs_0_, bf16[8,2176]{1,0:T(8,128)(2,1)S(1)} %collective-permute-done.refs_1_, ...), custom_call_target="tpu_custom_call" | custom-call | flops 201326592 | bytes 6291456 | tf_op jit(solution)/shard_map/pallas_call | solution.py:210
  15.3 0.0 collective-permute-start.8
  15.3 1.6 %collective-permute-start.9 = (bf16[32,1280]{1,0:T(8,128)(2,1)S(1)}, bf16[32,1280]{1,0:T(8,128)(2,1)S(1)}, u32[]{:S(2)}, u32[]{:S(2)}) collective-permute-start(bf16[32,1280]{1,0:T(8,128)(2,1)S(1)} %get-tuple-element.38), channel_id=1, source_target_pairs={{0,16},{8,24},{16,0},{24,8},{1,17},{9,25},{17,1},{25,9},{2,18},{10... | collective-permute-start | bytes 245768 | tf_op jit(solution)/shard_map/ppermute | solution.py:229
  16.9 0.3 collective-permute-start.10
  17.1 1.5 %collective-permute-start.3 = (bf16[32,128]{1,0:T(8,128)(2,1)S(1)}, bf16[32,128]{1,0:T(8,128)(2,1)S(1)}, u32[]{:S(2)}, u32[]{:S(2)}) collective-permute-start(bf16[32,128]{1,0:T(8,128)(2,1)S(1)} %get-tuple-element.30.gate_own), channel_id=1, source_target_pairs={{0,4},{4,0},{1,5},{5,1},{2,6},{6,2},{3,7},{7,3},{8,12},{12,8},{9,1... | collective-permute-start | bytes 24584 | tf_op jit(solution)/shard_map/ppermute | solution.py:229
  18.6 2.2 %collective-permute-done.3.gate_other = bf16[32,128]{1,0:T(8,128)(2,1)S(1)} collective-permute-done((bf16[32,128]{1,0:T(8,128)(2,1)S(1)}, bf16[32,128]{1,0:T(8,128)(2,1)S(1)}, u32[]{:S(2)}, u32[]{:S(2)}) %collective-permute-start.3) | collective-permute-done | bytes 8224 | tf_op jit(solution)/shard_map/ppermute | solution.py:229
  20.8 1.0 %shard_map.105 = (bf16[8,1152]{1,0:T(8,128)(2,1)S(1)}, bf16[8,1152]{1,0:T(8,128)(2,1)S(1)}, bf16[8,1152]{1,0:T(8,128)(2,1)S(1)}, bf16[8,1152]{1,0:T(8,128)(2,1)S(1)}) custom-call(bf16[32,1280]{1,0:T(8,128)(2,1)S(1)} %get-tuple-element.29.own.refs_0_, bf16[1,1,2048,768]{3,2,1,0:T(8,128)(2,1)S(1)} %get-tuple-element.27.refs_4_.up, ...), custom_call_target="tpu_custom_call" | custom-call | flops 100663296 | bytes 3145728 | tf_op jit(solution)/shard_map/pallas_call | solution.py:210
  21.8 1.6 %collective-permute-start.4 = (bf16[8,1152]{1,0:T(8,128)(2,1)S(1)}, bf16[8,1152]{1,0:T(8,128)(2,1)S(1)}, u32[]{:S(2)}, u32[]{:S(2)}) collective-permute-start(bf16[8,1152]{1,0:T(8,128)(2,1)S(1)} %get-tuple-element.31), channel_id=1, source_target_pairs={{0,4},{1,5},{2,6},{3,7},{4,0},{5,1},{6,2},{7,3},{8,12},{9,13},{10,... | collective-permute-start | bytes 55304 | tf_op jit(solution)/shard_map/ppermute | solution.py:229
  23.4 0.0 collective-permute-start.5
  23.4 2.3 %collective-permute-done.4.refs_0_ = bf16[8,1152]{1,0:T(8,128)(2,1)S(1)} collective-permute-done((bf16[8,1152]{1,0:T(8,128)(2,1)S(1)}, bf16[8,1152]{1,0:T(8,128)(2,1)S(1)}, u32[]{:S(2)}, u32[]{:S(2)}) %collective-permute-start.4) | collective-permute-done | bytes 18464 | tf_op jit(solution)/shard_map/ppermute | solution.py:229
  25.7 0.2 collective-permute-start.6
  25.9 2.2 %collective-permute-done.5.refs_1_ = bf16[8,1152]{1,0:T(8,128)(2,1)S(1)} collective-permute-done((bf16[8,1152]{1,0:T(8,128)(2,1)S(1)}, bf16[8,1152]{1,0:T(8,128)(2,1)S(1)}, u32[]{:S(2)}, u32[]{:S(2)}) %collective-permute-start.5) | collective-permute-done | bytes 18464 | tf_op jit(solution)/shard_map/ppermute | solution.py:229
  28.1 1.0 %collective-permute-start.7 = (bf16[8,1152]{1,0:T(8,128)(2,1)S(1)}, bf16[8,1152]{1,0:T(8,128)(2,1)S(1)}, u32[]{:S(2)}, u32[]{:S(2)}) collective-permute-start(bf16[8,1152]{1,0:T(8,128)(2,1)S(1)} %get-tuple-element.34), channel_id=1, source_target_pairs={{0,7},{1,6},{2,5},{3,4},{4,3},{5,2},{6,1},{7,0},{8,15},{9,14},{10,... | collective-permute-start | bytes 55304 | tf_op jit(solution)/shard_map/ppermute | solution.py:229
  29.0 2.2 %collective-permute-done.6.refs_2_ = bf16[8,1152]{1,0:T(8,128)(2,1)S(1)} collective-permute-done((bf16[8,1152]{1,0:T(8,128)(2,1)S(1)}, bf16[8,1152]{1,0:T(8,128)(2,1)S(1)}, u32[]{:S(2)}, u32[]{:S(2)}) %collective-permute-start.6) | collective-permute-done | bytes 18464 | tf_op jit(solution)/shard_map/ppermute | solution.py:229
  31.2 3.3 %collective-permute-done.7.refs_3_ = bf16[8,1152]{1,0:T(8,128)(2,1)S(1)} collective-permute-done((bf16[8,1152]{1,0:T(8,128)(2,1)S(1)}, bf16[8,1152]{1,0:T(8,128)(2,1)S(1)}, u32[]{:S(2)}, u32[]{:S(2)}) %collective-permute-start.7) | collective-permute-done | bytes 18464 | tf_op jit(solution)/shard_map/ppermute | solution.py:229
  34.5 1.2 %shard_map.106 = (bf16[1,128,2048]{2,1,0:T(8,128)(2,1)}, bf16[1,1,4,4]{3,2,1,0:T(4,128)(2,1)}) custom-call(bf16[8,1152]{1,0:T(8,128)(2,1)S(1)} %collective-permute-done.4.refs_0_, bf16[8,1152]{1,0:T(8,128)(2,1)S(1)} %collective-permute-done.5.refs_1_, bf16[8,1152]{1,0:T(8,128)(2,1)S(1)} %collective-permute-done.6.refs_2_, ...), custom_call_target="tpu_custom_call" | custom-call | flops 16777216 | bytes 524288 | tf_op jit(solution)/shard_map/pallas_call | solution.py:210
  35.7 0.0 collective-permute-done.8.refs_1_
  35.7 0.0 collective-permute-done.9.refs_2_
  35.7 0.0 collective-permute-done.10.refs_3_
  35.7 1.5 %shard_map.107 = (bf16[1,1,512,768]{3,2,1,0:T(8,128)(2,1)}, bf16[1,1,768,512]{3,2,1,0:T(8,128)(2,1)}) custom-call(bf16[32,1280]{1,0:T(8,128)(2,1)S(1)} %get-tuple-element.29.own.refs_0_, bf16[32,1280]{1,0:T(8,128)(2,1)S(1)} %collective-permute-done.8.refs_1_, bf16[32,1280]{1,0:T(8,128)(2,1)S(1)} %collective-permute-done.9.refs_2_, ...), custom_call_target="tpu_custom_call" | custom-call | flops 201326592 | bytes 1572864 | tf_op jit(solution)/shard_map/pallas_call | solution.py:210
Async XLA Ops:
  2.2 8.6 %collective-permute-start = (bf16[8,2176]{1,0:T(8,128)(2,1)S(1)}, bf16[8,2176]{1,0:T(8,128)(2,1)S(1)}, u32[]{:S(2)}, u32[]{:S(2)}) collective-permute-start(bf16[8,2176]{1,0:T(8,128)(2,1)S(1)} %get-tuple-element.24), channel_id=1, source_target_pairs={{0,1},{1,0},{2,3},{3,2},{4,5},{5,4},{6,7},{7,6},{8,9},{9,8},{10,11... | collective-permute-start | bytes 104456 | tf_op jit(solution)/shard_map/ppermute | solution.py:229
  5.3 5.5 %collective-permute-start.1 = (bf16[8,2176]{1,0:T(8,128)(2,1)S(1)}, bf16[8,2176]{1,0:T(8,128)(2,1)S(1)}, u32[]{:S(2)}, u32[]{:S(2)}) collective-permute-start(bf16[8,2176]{1,0:T(8,128)(2,1)S(1)} %get-tuple-element.25), channel_id=1, source_target_pairs={{0,2},{1,3},{2,0},{3,1},{4,6},{5,7},{6,4},{7,5},{8,10},{9,11},{10,... | collective-permute-start | bytes 104456 | tf_op jit(solution)/shard_map/ppermute | solution.py:229
  7.9 5.7 %collective-permute-start.2 = (bf16[8,2176]{1,0:T(8,128)(2,1)S(1)}, bf16[8,2176]{1,0:T(8,128)(2,1)S(1)}, u32[]{:S(2)}, u32[]{:S(2)}) collective-permute-start(bf16[8,2176]{1,0:T(8,128)(2,1)S(1)} %get-tuple-element.26), channel_id=1, source_target_pairs={{0,3},{1,2},{2,1},{3,0},{4,7},{5,6},{6,5},{7,4},{8,11},{9,10},{10,... | collective-permute-start | bytes 104456 | tf_op jit(solution)/shard_map/ppermute | solution.py:229
  15.3 20.4 %collective-permute-start.8 = (bf16[32,1280]{1,0:T(8,128)(2,1)S(1)}, bf16[32,1280]{1,0:T(8,128)(2,1)S(1)}, u32[]{:S(2)}, u32[]{:S(2)}) collective-permute-start(bf16[32,1280]{1,0:T(8,128)(2,1)S(1)} %get-tuple-element.37), channel_id=1, source_target_pairs={{0,8},{8,0},{16,24},{24,16},{1,9},{9,1},{17,25},{25,17},{2,10},{10... | collective-permute-start | bytes 245768 | tf_op jit(solution)/shard_map/ppermute | solution.py:229
  15.3 20.4 %collective-permute-start.9 = (bf16[32,1280]{1,0:T(8,128)(2,1)S(1)}, bf16[32,1280]{1,0:T(8,128)(2,1)S(1)}, u32[]{:S(2)}, u32[]{:S(2)}) collective-permute-start(bf16[32,1280]{1,0:T(8,128)(2,1)S(1)} %get-tuple-element.38), channel_id=1, source_target_pairs={{0,16},{8,24},{16,0},{24,8},{1,17},{9,25},{17,1},{25,9},{2,18},{10... | collective-permute-start | bytes 245768 | tf_op jit(solution)/shard_map/ppermute | solution.py:229
  16.9 18.8 %collective-permute-start.10 = (bf16[32,1280]{1,0:T(8,128)(2,1)S(1)}, bf16[32,1280]{1,0:T(8,128)(2,1)S(1)}, u32[]{:S(2)}, u32[]{:S(2)}) collective-permute-start(bf16[32,1280]{1,0:T(8,128)(2,1)S(1)} %get-tuple-element.39), channel_id=1, source_target_pairs={{0,24},{8,16},{16,8},{24,0},{1,25},{9,17},{17,9},{25,1},{2,26},{10... | collective-permute-start | bytes 245768 | tf_op jit(solution)/shard_map/ppermute | solution.py:229
  17.1 3.7 %collective-permute-start.3 = (bf16[32,128]{1,0:T(8,128)(2,1)S(1)}, bf16[32,128]{1,0:T(8,128)(2,1)S(1)}, u32[]{:S(2)}, u32[]{:S(2)}) collective-permute-start(bf16[32,128]{1,0:T(8,128)(2,1)S(1)} %get-tuple-element.30.gate_own), channel_id=1, source_target_pairs={{0,4},{4,0},{1,5},{5,1},{2,6},{6,2},{3,7},{7,3},{8,12},{12,8},{9,1... | collective-permute-start | bytes 24584 | tf_op jit(solution)/shard_map/ppermute | solution.py:229
  21.8 3.8 %collective-permute-start.4 = (bf16[8,1152]{1,0:T(8,128)(2,1)S(1)}, bf16[8,1152]{1,0:T(8,128)(2,1)S(1)}, u32[]{:S(2)}, u32[]{:S(2)}) collective-permute-start(bf16[8,1152]{1,0:T(8,128)(2,1)S(1)} %get-tuple-element.31), channel_id=1, source_target_pairs={{0,4},{1,5},{2,6},{3,7},{4,0},{5,1},{6,2},{7,3},{8,12},{9,13},{10,... | collective-permute-start | bytes 55304 | tf_op jit(solution)/shard_map/ppermute | solution.py:229
  23.4 4.7 %collective-permute-start.5 = (bf16[8,1152]{1,0:T(8,128)(2,1)S(1)}, bf16[8,1152]{1,0:T(8,128)(2,1)S(1)}, u32[]{:S(2)}, u32[]{:S(2)}) collective-permute-start(bf16[8,1152]{1,0:T(8,128)(2,1)S(1)} %get-tuple-element.32), channel_id=1, source_target_pairs={{0,5},{1,4},{2,7},{3,6},{4,1},{5,0},{6,3},{7,2},{8,13},{9,12},{10,... | collective-permute-start | bytes 55304 | tf_op jit(solution)/shard_map/ppermute | solution.py:229
  25.7 5.6 %collective-permute-start.6 = (bf16[8,1152]{1,0:T(8,128)(2,1)S(1)}, bf16[8,1152]{1,0:T(8,128)(2,1)S(1)}, u32[]{:S(2)}, u32[]{:S(2)}) collective-permute-start(bf16[8,1152]{1,0:T(8,128)(2,1)S(1)} %get-tuple-element.33), channel_id=1, source_target_pairs={{0,6},{1,7},{2,4},{3,5},{4,2},{5,3},{6,0},{7,1},{8,14},{9,15},{10,... | collective-permute-start | bytes 55304 | tf_op jit(solution)/shard_map/ppermute | solution.py:229
  28.1 6.5 %collective-permute-start.7 = (bf16[8,1152]{1,0:T(8,128)(2,1)S(1)}, bf16[8,1152]{1,0:T(8,128)(2,1)S(1)}, u32[]{:S(2)}, u32[]{:S(2)}) collective-permute-start(bf16[8,1152]{1,0:T(8,128)(2,1)S(1)} %get-tuple-element.34), channel_id=1, source_target_pairs={{0,7},{1,6},{2,5},{3,4},{4,3},{5,2},{6,1},{7,0},{8,15},{9,14},{10,... | collective-permute-start | bytes 55304 | tf_op jit(solution)/shard_map/ppermute | solution.py:229
where the time goes:
time: 37.4 us; the launch traced here: 37.3 us
  waiting for transfers between devices  15 us (40%)
  starting transfers between devices  11.8 us (32%)
  Pallas kernels  9.81 us (26%)
  between operations  0.69 us (2%)
    ppermute x11, waiting for transfers between devices, permuted(): return lax.ppermute(block, axes if len(axes) > 1 else axes[0], pairs)  15 us
    ppermute x11, starting transfers between devices, permuted(): return lax.ppermute(block, axes if len(axes) > 1 else axes[0], pairs)  11.8 us
    pallas_call x6, Pallas kernels, call(): pl.pallas_call(kernel, out_shape=out_shape, in_specs=[far_spec if k in fa...  9.81 us
  transfers between devices with their start and end apart: 11, of which 6 were waited for; matrix products, arithmetic and copies ran while one was open for 0% of the time, Pallas kernels for 14%

commit v1 on v0

--- a/solution.py
+++ b/solution.py
@@ -102,7 +102,7 @@
     blocks = blocks_of(refs[:n_blocks])
     up, down = refs[n_blocks : n_blocks + 2]
     outs = blocks_of(refs[n_blocks + 2 : -2])
-    gate_out, scaled = refs[-2:]
+    tail_out, scaled = refs[-2:]
     width, hidden_width = up.shape[2:]
     rows = 2 * capacity * len(blocks)
     part = width // replicas
@@ -123,30 +123,37 @@
     act_grad = prob * grad_proj * slope
     gate = jnp.sum(hidden * grad_proj, axis=1, keepdims=True)
     lane = lax.broadcasted_iota(jnp.int32, (rows, LANES), 1)
-    gate_out[...] = jnp.where(lane == 0, gate, tail).astype(BF16)
+    tail_out[...] = jnp.where(lane == 0, gate, tail).astype(BF16)
     _, _, first = row_marks(rows, hidden_width, capacity)
     both = jnp.where(first, act_grad, pltpu.roll(hidden, capacity, 0)).astype(BF16)
     place = own_place("dp", replicas)
     for k, out in enumerate(outs):
-        column = pl.multiple_of((place ^ k) * part, LANES)
+        wide = out.shape[1] - hidden_width
+        column = pl.multiple_of((place ^ k) // (wide // part) * wide, LANES)
         out[:, :hidden_width] = both
-        out[:, hidden_width:] = scaled[:, pl.ds(column, part)]
-
-
-def back_kernel(capacity, own, up, gate_own, gate_other, *outs):
+        out[:, hidden_width:] = scaled[:, pl.ds(column, wide)]
+
+
+def back_kernel(capacity, own, up, tail, out):
     width, hidden_width = up.shape[2:]
-    rows = own.shape[0]
     half = width // 2
     row_grad = lax.dot_general(
         own[:, :hidden_width], up[0, 0], (((1,), (1,)), ((), ())), preferred_element_type=F32
     )
-    _, _, first = row_marks(rows, half, capacity)
-    body = jnp.where(first, row_grad[:, :half], pltpu.roll(row_grad[:, half:], capacity, 0))
+    _, _, first = row_marks(own.shape[0], half, capacity)
+    upper = pltpu.roll(row_grad[:, half:], capacity, 0)
+    out[:, :half] = jnp.where(first, row_grad[:, :half], upper).astype(BF16)
+    out[:, half:] = tail[...]
+
+
+def reply_kernel(capacity, body, tail_own, *outs):
+    half = body.shape[1] - LANES
+    rows = body.shape[0]
     lane = lax.broadcasted_iota(jnp.int32, (rows, LANES), 1)
-    tail = jnp.where(lane == 0, gate_other[...].astype(F32), gate_own[...].astype(F32))
+    tail = jnp.where(lane == 0, tail_own[...].astype(F32), body[:, half:].astype(F32))
     size = 2 * capacity
     for k, out in enumerate(blocks_of(outs)):
-        out[:, :half] = body[k * size : (k + 1) * size].astype(BF16)
+        out[:, :half] = body[k * size : (k + 1) * size, :half]
         out[:, half:] = tail[k * size : (k + 1) * size].astype(BF16)
 
 
@@ -154,8 +161,16 @@
     blocks = blocks_of(refs[:n_blocks])
     grad_up, grad_down = refs[n_blocks:]
     hidden_width = grad_up.shape[3]
-    joined = jnp.concatenate([block[...] for block in blocks], axis=0)
-    both, sides = joined[:, :hidden_width], joined[:, hidden_width:]
+    part = grad_up.shape[2]
+    both = jnp.concatenate([block[:, :hidden_width] for block in blocks], axis=0)
+    columns = []
+    for block in blocks:
+        if block.shape[1] > hidden_width + part:
+            begin = hidden_width + (lax.axis_index("dp") & 1) * part
+            columns.append(block[:, pl.ds(pl.multiple_of(begin, LANES), part)])
+        else:
+            columns.append(block[:, hidden_width:])
+    sides = jnp.concatenate(columns, axis=0)
     _, _, first = row_marks(both.shape[0], both.shape[1], capacity)
     act_grad = jnp.where(first, both, jnp.zeros_like(both))
     grad_up[0, 0] = lax.dot_general(
@@ -246,14 +261,21 @@
     return [blocks[0]] + sent
 
 
-def sent_back(blocks, sections):
-    if len(blocks) == 1:
-        moved = permuted(blocks[0], ("pipe",), lambda p: ((p[0] - 1) % sections,))
-        return [lax.all_to_all(moved, "expert", split_axis=0, concat_axis=0, tiled=True)]
-    return [
-        permuted(b, ("pipe", "expert"), lambda p, k=k: ((p[0] - 1) % sections, p[1] ^ k))
-        for k, b in enumerate(blocks)
-    ]
+def share_shapes(replicas, rows, hidden_width, part):
+    if replicas != 4:
+        return message_shapes(replicas, rows, hidden_width + part)
+    widths = (hidden_width + part, hidden_width + part, hidden_width + 2 * part)
+    return [jax.ShapeDtypeStruct((rows, width), BF16) for width in widths]
+
+
+def shared(blocks, replicas):
+    if replicas != 4:
+        return exchanged(blocks, "dp")
+    own, near, far = blocks
+    crossed = permuted(far, ("dp",), lambda p: (p[0] ^ 2,))
+    beside = permuted(near, ("dp",), lambda p: (p[0] ^ 1,))
+    passed = permuted(crossed, ("dp",), lambda p: (p[0] ^ 1,))
+    return [own, beside, crossed, passed]
 
 
 def per_device(activations, out_grad, slot_token, slot_count, gate_prob, w_up, w_down):
@@ -288,25 +310,32 @@
     held = exchanged(packed, "expert")
     made = call(
         functools.partial(expert_kernel, capacity, replicas, len(held)),
-        message_shapes(replicas, rows, hidden_width + part)
+        share_shapes(replicas, rows, hidden_width, part)
         + [jax.ShapeDtypeStruct((rows, LANES), BF16)],
         (*held, near_up, near_down),
         4 * rows * width * hidden_width,
         4 * width * hidden_width,
         [pltpu.VMEM((rows, width), BF16)],
     )
-    shares, gate_own = made[:-1], made[-1]
-    gate_other = permuted(gate_own, ("pipe",), lambda p: ((p[0] + 1) % sections,))
-    joined = exchanged(shares, "dp")
+    shares, tail_own = made[:-1], made[-1]
+    joined = shared(shares, replicas)
     own = shares[0] if len(shares) > 1 else shares[0][0]
-    back = call(
+    (body,) = call(
         functools.partial(back_kernel, capacity),
-        message_shapes(experts, size, half + LANES),
-        (own, near_up, gate_own, gate_other),
+        [jax.ShapeDtypeStruct((rows, half + LANES), BF16)],
+        (own, near_up, tail_own),
         2 * rows * width * hidden_width,
         2 * width * hidden_width,
     )
-    returned = sent_back(back, sections)
+    body_after = permuted(body, ("pipe",), lambda p: ((p[0] - 1) % sections,))
+    replies = call(
+        functools.partial(reply_kernel, capacity),
+        message_shapes(experts, size, half + LANES),
+        (body_after, tail_own),
+        0,
+        4 * rows * half,
+    )
+    returned = exchanged(replies, "expert")
     grad_up, grad_down = call(
         functools.partial(weight_kernel, capacity, len(joined)),
         [

time: 37.4 us -> 36 us (0.963)
  waiting for transfers between devices: 15 us -> 11.8 us
  starting transfers between devices: 11.8 us -> 13.5 us
    ppermute x11 -> x10, waiting for transfers between devices: 15 us -> 11.8 us  [permuted(): return lax.ppermute(block, axes if len(axes) > 1 else axes[0], pairs)]
    ppermute x11 -> x10, starting transfers between devices: 11.8 us -> 13.5 us  [permuted(): return lax.ppermute(block, axes if len(axes) > 1 else axes[0], pairs)]
    pallas_call x6 -> x7, Pallas kernels: 9.81 us -> 9.84 us  [call(): pl.pallas_call(kernel, out_shape=out_shape, in_specs=[far_spec if k in fa...]
  transfers between devices with their start and end apart: 11 -> 10, of which waited for: 6 -> 5; matrix products, arithmetic and copies ran while one was open for 0% -> 0% of each run, Pallas kernels for 14% -> 14%
where the time goes in v1:
time: 36 us; the launch traced here: 35.8 us
  starting transfers between devices  13.5 us (38%)
  waiting for transfers between devices  11.8 us (33%)
  Pallas kernels  9.84 us (27%)
  between operations  0.69 us (2%)
    ppermute x10, starting transfers between devices, permuted(): return lax.ppermute(block, axes if len(axes) > 1 else axes[0], pairs)  13.5 us
    ppermute x10, waiting for transfers between devices, permuted(): return lax.ppermute(block, axes if len(axes) > 1 else axes[0], pairs)  11.8 us
    pallas_call x7, Pallas kernels, call(): pl.pallas_call(kernel, out_shape=out_shape, in_specs=[far_spec if k in fa...  9.84 us
  transfers between devices with their start and end apart: 10, of which 5 were waited for; matrix products, arithmetic and copies ran while one was open for 0% of the time, Pallas kernels for 14%

profile of v1, /device:TPU:0, one launch (start us, length us, event | category | flops | bytes accessed | tf_op | source)
XLA Modules:
  0.0 35.8 jit_solution(877896347597471627)
XLA Ops:
  0.6 1.6 %shard_map.102 = (bf16[8,2176]{1,0:T(8,128)(2,1)S(1)}, bf16[8,2176]{1,0:T(8,128)(2,1)S(1)}, bf16[8,2176]{1,0:T(8,128)(2,1)S(1)}, bf16[8,2176]{1,0:T(8,128)(2,1)S(1)}) custom-call(bf16[1,128,2048]{2,1,0:T(8,128)(2,1)} %acts_far.1, bf16[1,128,2048]{2,1,0:T(8,128)(2,1)} %grads_far.1, s32[1,1,4,4]{3,2,1,0:T(4,128)} %ids_far.1, s32[1,1,4]{2,1,0:T(1,128)} %counts_far.1, ...), custom_call_target="tpu_custom_call" | custom-call | flops 33554432 | bytes 1048576 | tf_op jit(solution)/shard_map/pallas_call | solution.py:225
  2.2 3.1 %collective-permute-start = (bf16[8,2176]{1,0:T(8,128)(2,1)S(1)}, bf16[8,2176]{1,0:T(8,128)(2,1)S(1)}, u32[]{:S(2)}, u32[]{:S(2)}) collective-permute-start(bf16[8,2176]{1,0:T(8,128)(2,1)S(1)} %get-tuple-element.23), channel_id=1, source_target_pairs={{0,1},{1,0},{2,3},{3,2},{4,5},{5,4},{6,7},{7,6},{8,9},{9,8},{10,11... | collective-permute-start | bytes 104456 | tf_op jit(solution)/shard_map/ppermute | solution.py:244
  5.3 2.6 %collective-permute-start.1 = (bf16[8,2176]{1,0:T(8,128)(2,1)S(1)}, bf16[8,2176]{1,0:T(8,128)(2,1)S(1)}, u32[]{:S(2)}, u32[]{:S(2)}) collective-permute-start(bf16[8,2176]{1,0:T(8,128)(2,1)S(1)} %get-tuple-element.24), channel_id=1, source_target_pairs={{0,2},{1,3},{2,0},{3,1},{4,6},{5,7},{6,4},{7,5},{8,10},{9,11},{10,... | collective-permute-start | bytes 104456 | tf_op jit(solution)/shard_map/ppermute | solution.py:244
  7.9 0.0 collective-permute-start.2
  7.9 2.9 %shard_map.103 = (bf16[1,1,2048,768]{3,2,1,0:T(8,128)(2,1)S(1)}, bf16[1,1,768,2048]{3,2,1,0:T(8,128)(2,1)S(1)}) custom-call(bf16[1,1,2048,768]{3,2,1,0:T(8,128)(2,1)} %up_far.1, bf16[1,1,768,2048]{3,2,1,0:T(8,128)(2,1)} %down_far.1, bf16[8,2176]{1,0:T(8,128)(2,1)S(1)} %get-tuple-element.22._.refs_0_), custom_call_target="tpu_custom_call" | custom-call | bytes 6291456 | tf_op jit(solution)/shard_map/pallas_call | solution.py:225
  10.8 0.0 collective-permute-done.refs_1_
  10.8 0.0 collective-permute-done.1.refs_2_
  10.8 2.8 %collective-permute-done.2.refs_3_ = bf16[8,2176]{1,0:T(8,128)(2,1)S(1)} collective-permute-done((bf16[8,2176]{1,0:T(8,128)(2,1)S(1)}, bf16[8,2176]{1,0:T(8,128)(2,1)S(1)}, u32[]{:S(2)}, u32[]{:S(2)}) %collective-permute-start.2) | collective-permute-done | bytes 34848 | tf_op jit(solution)/shard_map/ppermute | solution.py:244
  13.6 1.6 %shard_map.104 = (bf16[32,1280]{1,0:T(8,128)(2,1)S(1)}, bf16[32,1280]{1,0:T(8,128)(2,1)S(1)}, bf16[32,1792]{1,0:T(8,128)(2,1)S(1)}, bf16[32,128]{1,0:T(8,128)(2,1)S(1)}) custom-call(bf16[8,2176]{1,0:T(8,128)(2,1)S(1)} %get-tuple-element.22._.refs_0_, bf16[8,2176]{1,0:T(8,128)(2,1)S(1)} %collective-permute-done.refs_1_, ...), custom_call_target="tpu_custom_call" | custom-call | flops 201326592 | bytes 6291456 | tf_op jit(solution)/shard_map/pallas_call | solution.py:225
  15.3 1.5 %collective-permute-start.8 = (bf16[32,1792]{1,0:T(8,128)(2,1)S(1)}, bf16[32,1792]{1,0:T(8,128)(2,1)S(1)}, u32[]{:S(2)}, u32[]{:S(2)}) collective-permute-start(bf16[32,1792]{1,0:T(8,128)(2,1)S(1)} %get-tuple-element.37), channel_id=1, source_target_pairs={{0,16},{8,24},{16,0},{24,8},{1,17},{9,25},{17,1},{25,9},{2,18},{10... | collective-permute-start | bytes 344072 | tf_op jit(solution)/shard_map/ppermute | solution.py:244
  16.8 3.3 %collective-permute-done.8.refs_2_ = bf16[32,1792]{1,0:T(8,128)(2,1)S(1)} collective-permute-done((bf16[32,1792]{1,0:T(8,128)(2,1)S(1)}, bf16[32,1792]{1,0:T(8,128)(2,1)S(1)}, u32[]{:S(2)}, u32[]{:S(2)}) %collective-permute-start.8) | collective-permute-done | bytes 114720 | tf_op jit(solution)/shard_map/ppermute | solution.py:244
  20.1 0.0 collective-permute-start.9
  20.1 1.0 %shard_map.105 = bf16[32,1152]{1,0:T(8,128)(2,1)S(1)} custom-call(bf16[32,1280]{1,0:T(8,128)(2,1)S(1)} %get-tuple-element.28.own.refs_0_, bf16[1,1,2048,768]{3,2,1,0:T(8,128)(2,1)S(1)} %get-tuple-element.26.refs_4_.up, bf16[32,128]{1,0:T(8,128)(2,1)S(1)} %get-tuple-element.29.tail.tail_own), custom_call_target="tpu_custom_call" | custom-call | flops 100663296 | bytes 3145728 | tf_op jit(solution)/shard_map/pallas_call | solution.py:225
  21.1 1.6 %collective-permute-start.3 = (bf16[32,1152]{1,0:T(8,128)(2,1)S(1)}, bf16[32,1152]{1,0:T(8,128)(2,1)S(1)}, u32[]{:S(2)}, u32[]{:S(2)}) collective-permute-start(bf16[32,1152]{1,0:T(8,128)(2,1)S(1)} %shard_map.105), channel_id=1, source_target_pairs={{0,4},{4,0},{1,5},{5,1},{2,6},{6,2},{3,7},{7,3},{8,12},{12,8},{9,1... | collective-permute-start | bytes 221192 | tf_op jit(solution)/shard_map/ppermute | solution.py:244
  22.7 0.2 collective-permute-start.7
  22.9 3.0 %collective-permute-done.3.body = bf16[32,1152]{1,0:T(8,128)(2,1)S(1)} collective-permute-done((bf16[32,1152]{1,0:T(8,128)(2,1)S(1)}, bf16[32,1152]{1,0:T(8,128)(2,1)S(1)}, u32[]{:S(2)}, u32[]{:S(2)}) %collective-permute-start.3) | collective-permute-done | bytes 73760 | tf_op jit(solution)/shard_map/ppermute | solution.py:244
  25.9 0.1 collective-permute-start.4
  26.0 1.5 %collective-permute-start.5 = (bf16[8,1152]{1,0:T(8,128)(2,1)S(1)}, bf16[8,1152]{1,0:T(8,128)(2,1)S(1)}, u32[]{:S(2)}, u32[]{:S(2)}) collective-permute-start(bf16[8,1152]{1,0:T(8,128)(2,1)S(1)} %get-tuple-element.32), channel_id=1, source_target_pairs={{0,2},{1,3},{2,0},{3,1},{4,6},{5,7},{6,4},{7,5},{8,10},{9,11},{10,... | collective-permute-start | bytes 55304 | tf_op jit(solution)/shard_map/ppermute | solution.py:244
  27.5 2.8 %collective-permute-start.6 = (bf16[8,1152]{1,0:T(8,128)(2,1)S(1)}, bf16[8,1152]{1,0:T(8,128)(2,1)S(1)}, u32[]{:S(2)}, u32[]{:S(2)}) collective-permute-start(bf16[8,1152]{1,0:T(8,128)(2,1)S(1)} %get-tuple-element.33), channel_id=1, source_target_pairs={{0,3},{1,2},{2,1},{3,0},{4,7},{5,6},{6,5},{7,4},{8,11},{9,10},{10,... | collective-permute-start | bytes 55304 | tf_op jit(solution)/shard_map/ppermute | solution.py:244
  30.3 0.0 collective-permute-done.4.refs_1_
  30.3 0.3 collective-permute-done.5.refs_2_
  30.7 2.4 %collective-permute-done.6.refs_3_ = bf16[8,1152]{1,0:T(8,128)(2,1)S(1)} collective-permute-done((bf16[8,1152]{1,0:T(8,128)(2,1)S(1)}, bf16[8,1152]{1,0:T(8,128)(2,1)S(1)}, u32[]{:S(2)}, u32[]{:S(2)}) %collective-permute-start.6) | collective-permute-done | bytes 18464 | tf_op jit(solution)/shard_map/ppermute | solution.py:244
  33.1 1.2 %shard_map.107 = (bf16[1,128,2048]{2,1,0:T(8,128)(2,1)}, bf16[1,1,4,4]{3,2,1,0:T(4,128)(2,1)}) custom-call(bf16[8,1152]{1,0:T(8,128)(2,1)S(1)} %get-tuple-element.30.refs_0_, bf16[8,1152]{1,0:T(8,128)(2,1)S(1)} %collective-permute-done.4.refs_1_, bf16[8,1152]{1,0:T(8,128)(2,1)S(1)} %collective-permute-done.5.refs_2_, ...), custom_call_target="tpu_custom_call" | custom-call | flops 16777216 | bytes 524288 | tf_op jit(solution)/shard_map/pallas_call | solution.py:225
  34.3 0.0 collective-permute-done.7.refs_1_
  34.3 0.0 collective-permute-done.9.refs_3_
  34.3 1.5 %shard_map.108 = (bf16[1,1,512,768]{3,2,1,0:T(8,128)(2,1)}, bf16[1,1,768,512]{3,2,1,0:T(8,128)(2,1)}) custom-call(bf16[32,1280]{1,0:T(8,128)(2,1)S(1)} %get-tuple-element.28.own.refs_0_, bf16[32,1280]{1,0:T(8,128)(2,1)S(1)} %collective-permute-done.7.refs_1_, bf16[32,1792]{1,0:T(8,128)(2,1)S(1)} %collective-permute-done.8.refs_2_, ...), custom_call_target="tpu_custom_call" | custom-call | flops 201326592 | bytes 1572864 | tf_op jit(solution)/shard_map/pallas_call | solution.py:225
  (1 shorter events, 0.0 us)
Async XLA Ops:
  2.2 8.6 %collective-permute-start = (bf16[8,2176]{1,0:T(8,128)(2,1)S(1)}, bf16[8,2176]{1,0:T(8,128)(2,1)S(1)}, u32[]{:S(2)}, u32[]{:S(2)}) collective-permute-start(bf16[8,2176]{1,0:T(8,128)(2,1)S(1)} %get-tuple-element.23), channel_id=1, source_target_pairs={{0,1},{1,0},{2,3},{3,2},{4,5},{5,4},{6,7},{7,6},{8,9},{9,8},{10,11... | collective-permute-start | bytes 104456 | tf_op jit(solution)/shard_map/ppermute | solution.py:244
  5.3 5.5 %collective-permute-start.1 = (bf16[8,2176]{1,0:T(8,128)(2,1)S(1)}, bf16[8,2176]{1,0:T(8,128)(2,1)S(1)}, u32[]{:S(2)}, u32[]{:S(2)}) collective-permute-start(bf16[8,2176]{1,0:T(8,128)(2,1)S(1)} %get-tuple-element.24), channel_id=1, source_target_pairs={{0,2},{1,3},{2,0},{3,1},{4,6},{5,7},{6,4},{7,5},{8,10},{9,11},{10,... | collective-permute-start | bytes 104456 | tf_op jit(solution)/shard_map/ppermute | solution.py:244
  7.9 5.7 %collective-permute-start.2 = (bf16[8,2176]{1,0:T(8,128)(2,1)S(1)}, bf16[8,2176]{1,0:T(8,128)(2,1)S(1)}, u32[]{:S(2)}, u32[]{:S(2)}) collective-permute-start(bf16[8,2176]{1,0:T(8,128)(2,1)S(1)} %get-tuple-element.25), channel_id=1, source_target_pairs={{0,3},{1,2},{2,1},{3,0},{4,7},{5,6},{6,5},{7,4},{8,11},{9,10},{10,... | collective-permute-start | bytes 104456 | tf_op jit(solution)/shard_map/ppermute | solution.py:244
  15.3 4.8 %collective-permute-start.8 = (bf16[32,1792]{1,0:T(8,128)(2,1)S(1)}, bf16[32,1792]{1,0:T(8,128)(2,1)S(1)}, u32[]{:S(2)}, u32[]{:S(2)}) collective-permute-start(bf16[32,1792]{1,0:T(8,128)(2,1)S(1)} %get-tuple-element.37), channel_id=1, source_target_pairs={{0,16},{8,24},{16,0},{24,8},{1,17},{9,25},{17,1},{25,9},{2,18},{10... | collective-permute-start | bytes 344072 | tf_op jit(solution)/shard_map/ppermute | solution.py:244
  20.1 14.2 %collective-permute-start.9 = (bf16[32,1792]{1,0:T(8,128)(2,1)S(1)}, bf16[32,1792]{1,0:T(8,128)(2,1)S(1)}, u32[]{:S(2)}, u32[]{:S(2)}) collective-permute-start(bf16[32,1792]{1,0:T(8,128)(2,1)S(1)} %collective-permute-done.8.refs_2_), channel_id=1, source_target_pairs={{0,8},{8,0},{16,24},{24,16},{1,9},{9,1},{17,25},{25,17},{2,10},{10... | collective-permute-start | bytes 344072 | tf_op jit(solution)/shard_map/ppermute | solution.py:244
  21.1 4.7 %collective-permute-start.3 = (bf16[32,1152]{1,0:T(8,128)(2,1)S(1)}, bf16[32,1152]{1,0:T(8,128)(2,1)S(1)}, u32[]{:S(2)}, u32[]{:S(2)}) collective-permute-start(bf16[32,1152]{1,0:T(8,128)(2,1)S(1)} %shard_map.105), channel_id=1, source_target_pairs={{0,4},{4,0},{1,5},{5,1},{2,6},{6,2},{3,7},{7,3},{8,12},{12,8},{9,1... | collective-permute-start | bytes 221192 | tf_op jit(solution)/shard_map/ppermute | solution.py:244
  22.7 11.6 %collective-permute-start.7 = (bf16[32,1280]{1,0:T(8,128)(2,1)S(1)}, bf16[32,1280]{1,0:T(8,128)(2,1)S(1)}, u32[]{:S(2)}, u32[]{:S(2)}) collective-permute-start(bf16[32,1280]{1,0:T(8,128)(2,1)S(1)} %get-tuple-element.36), channel_id=1, source_target_pairs={{0,8},{8,0},{16,24},{24,16},{1,9},{9,1},{17,25},{25,17},{2,10},{10... | collective-permute-start | bytes 245768 | tf_op jit(solution)/shard_map/ppermute | solution.py:244
  25.9 4.5 %collective-permute-start.4 = (bf16[8,1152]{1,0:T(8,128)(2,1)S(1)}, bf16[8,1152]{1,0:T(8,128)(2,1)S(1)}, u32[]{:S(2)}, u32[]{:S(2)}) collective-permute-start(bf16[8,1152]{1,0:T(8,128)(2,1)S(1)} %get-tuple-element.31), channel_id=1, source_target_pairs={{0,1},{1,0},{2,3},{3,2},{4,5},{5,4},{6,7},{7,6},{8,9},{9,8},{10,11... | collective-permute-start | bytes 55304 | tf_op jit(solution)/shard_map/ppermute | solution.py:244
  26.0 4.7 %collective-permute-start.5 = (bf16[8,1152]{1,0:T(8,128)(2,1)S(1)}, bf16[8,1152]{1,0:T(8,128)(2,1)S(1)}, u32[]{:S(2)}, u32[]{:S(2)}) collective-permute-start(bf16[8,1152]{1,0:T(8,128)(2,1)S(1)} %get-tuple-element.32), channel_id=1, source_target_pairs={{0,2},{1,3},{2,0},{3,1},{4,6},{5,7},{6,4},{7,5},{8,10},{9,11},{10,... | collective-permute-start | bytes 55304 | tf_op jit(solution)/shard_map/ppermute | solution.py:244
  27.5 5.6 %collective-permute-start.6 = (bf16[8,1152]{1,0:T(8,128)(2,1)S(1)}, bf16[8,1152]{1,0:T(8,128)(2,1)S(1)}, u32[]{:S(2)}, u32[]{:S(2)}) collective-permute-start(bf16[8,1152]{1,0:T(8,128)(2,1)S(1)} %get-tuple-element.33), channel_id=1, source_target_pairs={{0,3},{1,2},{2,1},{3,0},{4,7},{5,6},{6,5},{7,4},{8,11},{9,10},{10,... | collective-permute-start | bytes 55304 | tf_op jit(solution)/shard_map/ppermute | solution.py:244

commit v2 on v1

--- a/solution.py
+++ b/solution.py
@@ -12,8 +12,8 @@
 BF16 = jnp.bfloat16
 F32 = jnp.float32
 LANES = 128
-PERMUTE_LIMIT = 4
 KERNEL_VMEM = 24 << 20
+PIECES = 2
 
 
 def row_marks(rows, width, capacity):
@@ -33,25 +33,38 @@
     return list(refs)
 
 
-def own_place(axis, size):
-    return lax.axis_index(axis) if size <= PERMUTE_LIMIT else 0
+def in_pairs(experts, replicas):
+    return experts == 4 and replicas == 4
+
+
+def partner_of(group, low_first):
+    side = (lax.axis_index("dp") & 1) ^ lax.shift_right_logical(group, 1)
+    high = group & 1 if low_first else 1 - (group & 1)
+    return 2 * high + side
 
 
 def pack_kernel(acts_far, grads_far, ids_far, counts_far, probs_far, *refs):
     outs, acts, grads, ids, counts, probs, sems = refs[:-6], *refs[-6:]
-    near = (ids, counts, probs, acts, grads)
-    far = (ids_far, counts_far, probs_far, acts_far, grads_far)
-    copies = [pltpu.make_async_copy(a, b, sems.at[k]) for k, (a, b) in enumerate(zip(far, near))]
+    tokens, width = acts.shape[1:]
+    spans = [pl.ds(k * width // PIECES, width // PIECES) for k in range(PIECES)]
+    pairs = [(ids_far, ids), (counts_far, counts), (probs_far, probs)]
+    for span in spans:
+        pairs.append((acts_far.at[:, :, span], acts.at[:, :, span]))
+        pairs.append((grads_far.at[:, :, span], grads.at[:, :, span]))
+    copies = [pltpu.make_async_copy(a, b, sems.at[k]) for k, (a, b) in enumerate(pairs)]
     for copy in copies:
         copy.start()
     for copy in copies[:3]:
         copy.wait()
-    tokens, width = acts.shape[1:]
     experts, capacity = ids.shape[2:]
     rows = 2 * experts * capacity
-    place = own_place("expert", experts)
+    paired = in_pairs(experts, lax.axis_size("dp"))
+
+    def dest_of(group):
+        return partner_of(group, True) ^ lax.axis_index("expert") if paired else group
+
     group, slot, _ = row_marks(rows, capacity, capacity)
-    dest = group ^ place
+    dest = dest_of(group)
     id_rows = ids[0, 0].astype(F32)
     prob_rows = probs[0, 0].astype(F32)
     id_grid = jnp.zeros((rows, capacity), F32)
@@ -63,7 +76,7 @@
     at_slot = lax.broadcasted_iota(jnp.int32, (rows, capacity), 1) == slot
     id_col = jnp.sum(jnp.where(at_slot, id_grid, 0.0), axis=1, keepdims=True)
     prob_col = jnp.sum(jnp.where(at_slot, prob_grid, 0.0), axis=1, keepdims=True)
-    dest_wide = row_marks(rows, experts, capacity)[0] ^ place
+    dest_wide = dest_of(row_marks(rows, experts, capacity)[0])
     at_dest = lax.broadcasted_iota(jnp.int32, (rows, experts), 1) == dest_wide
     count_row = counts[0].astype(F32)
     count_col = jnp.sum(jnp.where(at_dest, count_row, 0.0), axis=1, keepdims=True)
@@ -75,16 +88,35 @@
     hit_live = jnp.where(live, hit, 0.0)
     pick_act = jnp.where(first_wide, hit, 0.0).astype(BF16)
     pick_grad = jnp.where(first_wide, 0.0, hit_live).astype(BF16)
-    for copy in copies[3:]:
-        copy.wait()
-    picked = jnp.dot(pick_act, acts[0], preferred_element_type=F32)
-    picked = picked + jnp.dot(pick_grad, grads[0], preferred_element_type=F32)
     tail_lane = lax.broadcasted_iota(jnp.int32, (rows, LANES), 1)
     tail = jnp.where(tail_lane == 0, prob_col, jnp.where(tail_lane == 1, id_col, 0.0))
-    size = 2 * capacity
-    for k, out in enumerate(blocks_of(outs)):
-        out[:, :width] = picked[k * size : (k + 1) * size].astype(BF16)
+    blocks = blocks_of(outs)
+    size = rows // len(blocks)
+    for k, out in enumerate(blocks):
         out[:, width:] = tail[k * size : (k + 1) * size].astype(BF16)
+    for piece, span in enumerate(spans):
+        copies[3 + 2 * piece].wait()
+        picked = jnp.dot(pick_act, acts[0, :, span], preferred_element_type=F32)
+        copies[4 + 2 * piece].wait()
+        picked = picked + jnp.dot(pick_grad, grads[0, :, span], preferred_element_type=F32)
+        for k, out in enumerate(blocks):
+            out[:, span] = picked[k * size : (k + 1) * size].astype(BF16)
+
+
+def halves(ref):
+    value = ref[...].astype(F32)
+    size = ref.shape[0] // 2
+    return value[:size], value[size:]
+
+
+def join_kernel(kept, came, high, low):
+    (kept_low, kept_high), (came_low, came_high) = halves(kept), halves(came)
+    high[...] = jnp.concatenate([kept_high, came_high], axis=0).astype(BF16)
+    low[...] = jnp.concatenate([kept_low, came_low], axis=0).astype(BF16)
+
+
+def other_kernel(high, low, out):
+    out[...] = jnp.concatenate([halves(high)[1], halves(low)[1]], axis=0).astype(BF16)
 
 
 def load_kernel(up_far, down_far, _, up, down, sems):
@@ -104,7 +136,7 @@
     outs = blocks_of(refs[n_blocks + 2 : -2])
     tail_out, scaled = refs[-2:]
     width, hidden_width = up.shape[2:]
-    rows = 2 * capacity * len(blocks)
+    rows = sum(block.shape[0] for block in blocks)
     part = width // replicas
     packed = stacked_rows(blocks, 0, width)
     tail = stacked_rows(blocks, width, width + LANES)
@@ -126,7 +158,7 @@
     tail_out[...] = jnp.where(lane == 0, gate, tail).astype(BF16)
     _, _, first = row_marks(rows, hidden_width, capacity)
     both = jnp.where(first, act_grad, pltpu.roll(hidden, capacity, 0)).astype(BF16)
-    place = own_place("dp", replicas)
+    place = lax.axis_index("dp") if replicas == 4 else 0
     for k, out in enumerate(outs):
         wide = out.shape[1] - hidden_width
         column = pl.multiple_of((place ^ k) // (wide // part) * wide, LANES)
@@ -134,7 +166,7 @@
         out[:, hidden_width:] = scaled[:, pl.ds(column, wide)]
 
 
-def back_kernel(capacity, own, up, tail, out):
+def back_kernel(capacity, own, up, body):
     width, hidden_width = up.shape[2:]
     half = width // 2
     row_grad = lax.dot_general(
@@ -142,18 +174,17 @@
     )
     _, _, first = row_marks(own.shape[0], half, capacity)
     upper = pltpu.roll(row_grad[:, half:], capacity, 0)
-    out[:, :half] = jnp.where(first, row_grad[:, :half], upper).astype(BF16)
-    out[:, half:] = tail[...]
-
-
-def reply_kernel(capacity, body, tail_own, *outs):
-    half = body.shape[1] - LANES
-    rows = body.shape[0]
+    body[...] = jnp.where(first, row_grad[:, :half], upper).astype(BF16)
+
+
+def reply_kernel(body, tail_own, tail_other, *outs):
+    rows, half = body.shape
     lane = lax.broadcasted_iota(jnp.int32, (rows, LANES), 1)
-    tail = jnp.where(lane == 0, tail_own[...].astype(F32), body[:, half:].astype(F32))
-    size = 2 * capacity
-    for k, out in enumerate(blocks_of(outs)):
-        out[:, :half] = body[k * size : (k + 1) * size, :half]
+    tail = jnp.where(lane == 0, tail_other[...].astype(F32), tail_own[...].astype(F32))
+    blocks = blocks_of(outs)
+    size = rows // len(blocks)
+    for k, out in enumerate(blocks):
+        out[:, :half] = body[k * size : (k + 1) * size]
         out[:, half:] = tail[k * size : (k + 1) * size].astype(BF16)
 
 
@@ -185,48 +216,64 @@
 
 def combine_kernel(capacity, sections, n_blocks, *refs):
     blocks = blocks_of(refs[:n_blocks])
-    grad_prev, grad_gate = refs[n_blocks:]
-    tokens, width = grad_prev.shape[1:]
-    experts = len(blocks)
+    up_near, down_near, prev_far, gate_far, up_far, down_far, prev, gate, sems = refs[n_blocks:]
+    tokens, width = prev.shape[1:]
+    experts = gate.shape[2]
+    paired = in_pairs(experts, lax.axis_size("dp"))
     half = width // 2
     rows = 2 * capacity * experts
-    body = stacked_rows(blocks, 0, half).astype(BF16)
-    tail = stacked_rows(blocks, half, half + LANES)
+    spans = [pl.ds(k * half, half) for k in range(2)]
+    pairs = [(prev.at[:, :, span], prev_far.at[:, :, span]) for span in spans]
+    pairs += [(gate, gate_far), (up_near, up_far), (down_near, down_far)]
+    copies = [pltpu.make_async_copy(a, b, sems.at[k]) for k, (a, b) in enumerate(pairs)]
+    copies[3].start()
+    copies[4].start()
+    if paired:
+        high, low, came = blocks
+        joined = jnp.concatenate([halves(high)[0], halves(low)[0], *halves(came)], axis=0)
+    else:
+        joined = stacked_rows(blocks, 0, half + LANES)
+    body, tail = joined[:, :half].astype(BF16), joined[:, half:]
     _, _, first = row_marks(rows, tokens, capacity)
     lane = lax.broadcasted_iota(jnp.int32, (rows, tokens), 1).astype(F32)
     kept = jnp.where(lax.axis_index("pipe") == sections - 1, 0.0, 1.0)
     hit = jnp.where(lane == tail[:, 1:2], kept, 0.0)
     for part, mark in enumerate((first, jnp.logical_not(first))):
         one_hot = jnp.where(mark, hit, 0.0).astype(BF16)
-        grad_prev[0, :, part * half : (part + 1) * half] = lax.dot_general(
+        prev[0, :, spans[part]] = lax.dot_general(
             one_hot, body, (((0,), (0,)), ((), ())), preferred_element_type=F32
         ).astype(BF16)
+        copies[part].start()
     _, slot, first = row_marks(rows, capacity, capacity)
     at_slot = lax.broadcasted_iota(jnp.int32, (rows, capacity), 1) == slot
     gates = jnp.where(jnp.logical_and(at_slot, first), tail[:, 0:1], 0.0).astype(BF16)
     column = lax.broadcasted_iota(jnp.int32, (experts, rows), 1)
     source = lax.shift_right_logical(column, (2 * capacity).bit_length() - 1)
-    source = source ^ own_place("expert", experts)
+    if paired:
+        source = partner_of(source, False) ^ lax.axis_index("expert")
     wanted = source == lax.broadcasted_iota(jnp.int32, (experts, rows), 0)
-    grad_gate[0, 0] = jnp.dot(
+    gate[0, 0] = jnp.dot(
         jnp.where(wanted, 1.0, 0.0).astype(BF16), gates, preferred_element_type=F32
     ).astype(BF16)
-
-
-def call(kernel, out_shape, args, flops, n_bytes, scratch=(), far=(), near_out=True):
+    copies[2].start()
+    for copy in copies:
+        copy.wait()
+
+
+def call(kernel, out_shape, args, flops, n_bytes, scratch=(), far=(), far_out=False):
     near_spec = pl.BlockSpec(memory_space=pltpu.VMEM)
     far_spec = pl.BlockSpec(memory_space=pl.ANY)
     args = [
         pltpu.with_memory_space_constraint(a, pltpu.HBM if k in far else pltpu.VMEM)
         for k, a in enumerate(args)
     ]
-    if near_out:
+    if not far_out:
         out_shape = [pltpu.VMEM(s.shape, s.dtype) for s in out_shape]
     return pl.pallas_call(
         kernel,
         out_shape=out_shape,
         in_specs=[far_spec if k in far else near_spec for k in range(len(args))],
-        out_specs=[near_spec] * len(out_shape),
+        out_specs=[far_spec if far_out else near_spec] * len(out_shape),
         scratch_shapes=list(scratch),
         compiler_params=pltpu.CompilerParams(vmem_limit_bytes=KERNEL_VMEM),
         cost_estimate=pl.CostEstimate(flops=flops, bytes_accessed=n_bytes, transcendentals=0),
@@ -244,37 +291,34 @@
     return lax.ppermute(block, axes if len(axes) > 1 else axes[0], pairs)
 
 
-def message_shapes(count, rows, width):
-    if count <= PERMUTE_LIMIT:
-        return [jax.ShapeDtypeStruct((rows, width), BF16)] * count
+def message_shapes(paired, count, rows, width):
+    if paired:
+        return [jax.ShapeDtypeStruct((count * rows // 2, width), BF16)] * 2
     return [jax.ShapeDtypeStruct((count, rows, width), BF16)]
 
 
-def exchanged(blocks, axis):
-    if len(blocks) == 1:
-        return [lax.all_to_all(blocks[0], axis, split_axis=0, concat_axis=0, tiled=True)]
-    sent = [
-        permuted(b, (axis,), lambda p, k=k: (p[0] ^ k,))
-        for k, b in enumerate(blocks)
-        if k
-    ]
-    return [blocks[0]] + sent
+def traded(block, axis):
+    return lax.all_to_all(block, axis, split_axis=0, concat_axis=0, tiled=True)
+
+
+def swapped(block):
+    return permuted(block, ("dp",), lambda p: (p[0] ^ 1,))
 
 
 def share_shapes(replicas, rows, hidden_width, part):
     if replicas != 4:
-        return message_shapes(replicas, rows, hidden_width + part)
+        return message_shapes(False, replicas, rows, hidden_width + part)
     widths = (hidden_width + part, hidden_width + part, hidden_width + 2 * part)
     return [jax.ShapeDtypeStruct((rows, width), BF16) for width in widths]
 
 
 def shared(blocks, replicas):
     if replicas != 4:
-        return exchanged(blocks, "dp")
+        return [traded(blocks[0], "dp")]
     own, near, far = blocks
     crossed = permuted(far, ("dp",), lambda p: (p[0] ^ 2,))
-    beside = permuted(near, ("dp",), lambda p: (p[0] ^ 1,))
-    passed = permuted(crossed, ("dp",), lambda p: (p[0] ^ 1,))
+    beside = swapped(near)
+    passed = swapped(crossed)
     return [own, beside, crossed, passed]
 
 
@@ -288,14 +332,15 @@
     rows = size * experts
     part = width // replicas
     half = width // 2
+    paired = in_pairs(experts, replicas)
     sources = (activations, out_grad, slot_token, slot_count, gate_prob)
     packed = call(
         pack_kernel,
-        message_shapes(experts, size, width + LANES),
+        message_shapes(paired, experts, size, width + LANES),
         sources,
         4 * rows * tokens * width,
         4 * tokens * width,
-        [pltpu.VMEM(a.shape, a.dtype) for a in sources] + [pltpu.SemaphoreType.DMA((5,))],
+        [pltpu.VMEM(a.shape, a.dtype) for a in sources] + [pltpu.SemaphoreType.DMA((3 + 2 * PIECES,))],
         far=range(5),
     )
     near_up, near_down = call(
@@ -307,7 +352,21 @@
         [pltpu.SemaphoreType.DMA((2,))],
         far=range(2),
     )
-    held = exchanged(packed, "expert")
+    if paired:
+        kept, sent = packed
+        high, low = call(
+            join_kernel,
+            message_shapes(paired, experts, size, width + LANES),
+            (kept, swapped(sent)),
+            0,
+            4 * rows * width,
+        )
+        held = [
+            permuted(high, ("dp", "expert"), lambda p: (p[0], p[1] ^ 2 ^ (p[0] & 1))),
+            permuted(low, ("dp", "expert"), lambda p: (p[0], p[1] ^ (p[0] & 1))),
+        ]
+    else:
+        held = [traded(packed[0], "expert")]
     made = call(
         functools.partial(expert_kernel, capacity, replicas, len(held)),
         share_shapes(replicas, rows, hidden_width, part)
@@ -320,43 +379,63 @@
     shares, tail_own = made[:-1], made[-1]
     joined = shared(shares, replicas)
     own = shares[0] if len(shares) > 1 else shares[0][0]
+    tail_other = permuted(tail_own, ("pipe",), lambda p: ((p[0] + 1) % sections,))
     (body,) = call(
         functools.partial(back_kernel, capacity),
-        [jax.ShapeDtypeStruct((rows, half + LANES), BF16)],
-        (own, near_up, tail_own),
+        [jax.ShapeDtypeStruct((rows, half), BF16)],
+        (own, near_up),
         2 * rows * width * hidden_width,
         2 * width * hidden_width,
     )
-    body_after = permuted(body, ("pipe",), lambda p: ((p[0] - 1) % sections,))
     replies = call(
-        functools.partial(reply_kernel, capacity),
-        message_shapes(experts, size, half + LANES),
-        (body_after, tail_own),
+        reply_kernel,
+        message_shapes(paired, experts, size, half + LANES),
+        (body, tail_own, tail_other),
         0,
         4 * rows * half,
     )
-    returned = exchanged(replies, "expert")
-    grad_up, grad_down = call(
+    if paired:
+        every = ("dp", "pipe", "expert")
+
+        def before(p, step):
+            return (p[0], (p[1] - 1) % sections, p[2] ^ step ^ (p[0] & 1))
+
+        high = permuted(replies[0], every, lambda p: before(p, 2))
+        low = permuted(replies[1], every, lambda p: before(p, 0))
+        (other,) = call(
+            other_kernel,
+            [jax.ShapeDtypeStruct((rows // 2, half + LANES), BF16)],
+            (high, low),
+            0,
+            4 * rows * half,
+        )
+        returned = [high, low, swapped(other)]
+    else:
+        moved = permuted(replies[0], ("pipe",), lambda p: ((p[0] - 1) % sections,))
+        returned = [traded(moved, "expert")]
+    weight_grads = [
+        jax.ShapeDtypeStruct((1, 1, part, hidden_width), BF16),
+        jax.ShapeDtypeStruct((1, 1, hidden_width, part), BF16),
+    ]
+    near_grads = call(
         functools.partial(weight_kernel, capacity, len(joined)),
-        [
-            jax.ShapeDtypeStruct((1, 1, part, hidden_width), BF16),
-            jax.ShapeDtypeStruct((1, 1, hidden_width, part), BF16),
-        ],
+        weight_grads,
         tuple(joined),
         4 * replicas * rows * part * hidden_width,
         4 * part * hidden_width,
-        near_out=False,
-    )
-    grad_prev, grad_gate = call(
+    )
+    token_grads = [
+        jax.ShapeDtypeStruct((1, tokens, width), BF16),
+        jax.ShapeDtypeStruct((1, 1, experts, capacity), BF16),
+    ]
+    grad_prev, grad_gate, grad_up, grad_down = call(
         functools.partial(combine_kernel, capacity, sections, len(returned)),
-        [
-            jax.ShapeDtypeStruct((1, tokens, width), BF16),
-            jax.ShapeDtypeStruct((1, 1, experts, capacity), BF16),
-        ],
-        tuple(returned),
+        token_grads + weight_grads,
+        (*returned, *near_grads),
         2 * rows * tokens * width,
         2 * tokens * width,
-        near_out=False,
+        [pltpu.VMEM(s.shape, s.dtype) for s in token_grads] + [pltpu.SemaphoreType.DMA((5,))],
+        far_out=True,
     )
     return grad_prev, grad_gate, grad_up, grad_down
 

time: 36 us -> 32.9 us (0.914)
  starting transfers between devices: 13.5 us -> 12.2 us
  waiting for transfers between devices: 11.8 us -> 10.7 us
  Pallas kernels: 9.84 us -> 9.1 us
    ppermute x10, starting transfers between devices: 13.5 us -> 12.2 us  [permuted(): return lax.ppermute(block, axes if len(axes) > 1 else axes[0], pairs)]
    ppermute x10, waiting for transfers between devices: 11.8 us -> 10.7 us  [permuted(): return lax.ppermute(block, axes if len(axes) > 1 else axes[0], pairs)]
    pallas_call x7 -> x9, Pallas kernels: 9.84 us -> 9.1 us  [call(): pl.pallas_call(kernel, out_shape=out_shape, in_specs=[far_spec if k in fa...]
  transfers between devices with their start and end apart: 10 -> 10, of which waited for: 5 -> 7; matrix products, arithmetic and copies ran while one was open for 0% -> 0% of each run, Pallas kernels for 14% -> 14%
where the time goes in v2:
time: 32.9 us; the launch traced here: 32.7 us
  starting transfers between devices  12.2 us (37%)
  waiting for transfers between devices  10.7 us (33%)
  Pallas kernels  9.1 us (28%)
  between operations  0.7 us (2%)
    ppermute x10, starting transfers between devices, permuted(): return lax.ppermute(block, axes if len(axes) > 1 else axes[0], pairs)  12.2 us
    ppermute x10, waiting for transfers between devices, permuted(): return lax.ppermute(block, axes if len(axes) > 1 else axes[0], pairs)  10.7 us
    pallas_call x9, Pallas kernels, call(): pl.pallas_call(kernel, out_shape=out_shape, in_specs=[far_spec if k in fa...  9.1 us
  transfers between devices with their start and end apart: 10, of which 7 were waited for; matrix products, arithmetic and copies ran while one was open for 0% of the time, Pallas kernels for 14%

profile of v2, /device:TPU:0, one launch (start us, length us, event | category | flops | bytes accessed | tf_op | source)
XLA Modules:
  0.0 32.7 jit_solution(14699932481675252860)
XLA Ops:
  0.6 1.6 %shard_map.102 = (bf16[16,2176]{1,0:T(8,128)(2,1)S(1)}, bf16[16,2176]{1,0:T(8,128)(2,1)S(1)}) custom-call(bf16[1,128,2048]{2,1,0:T(8,128)(2,1)} %acts_far.1, bf16[1,128,2048]{2,1,0:T(8,128)(2,1)} %grads_far.1, s32[1,1,4,4]{3,2,1,0:T(4,128)} %ids_far.1, s32[1,1,4]{2,1,0:T(1,128)} %counts_far.1, bf16[1,1,4,4]{3,2,1,0:T(4,128)(2,1)} %probs_far.1), custom_call_target="tpu_custom_call" | custom-call | flops 33554432 | bytes 1048576 | tf_op jit(solution)/shard_map/pallas_call | solution.py:272
  2.2 0.6 %collective-permute-start = (bf16[16,2176]{1,0:T(8,128)(2,1)S(1)}, bf16[16,2176]{1,0:T(8,128)(2,1)S(1)}, u32[]{:S(2)}, u32[]{:S(2)}) collective-permute-start(bf16[16,2176]{1,0:T(8,128)(2,1)S(1)} %get-tuple-element.19), channel_id=1, source_target_pairs={{0,8},{8,0},{16,24},{24,16},{1,9},{9,1},{17,25},{25,17},{2,10},{10... | collective-permute-start | bytes 208904 | tf_op jit(solution)/shard_map/ppermute | solution.py:291
  2.8 0.9 %collective-permute-done.came = bf16[16,2176]{1,0:T(8,128)(2,1)S(1)} collective-permute-done((bf16[16,2176]{1,0:T(8,128)(2,1)S(1)}, bf16[16,2176]{1,0:T(8,128)(2,1)S(1)}, u32[]{:S(2)}, u32[]{:S(2)}) %collective-permute-start) | collective-permute-done | bytes 69664 | tf_op jit(solution)/shard_map/ppermute | solution.py:291
  3.7 4.0 %collective-permute-start.1 = (bf16[16,2176]{1,0:T(8,128)(2,1)S(1)}, bf16[16,2176]{1,0:T(8,128)(2,1)S(1)}, u32[]{:S(2)}, u32[]{:S(2)}) collective-permute-start(bf16[16,2176]{1,0:T(8,128)(2,1)S(1)} %get-tuple-element.20), channel_id=1, source_target_pairs={{0,2},{1,3},{2,0},{3,1},{8,11},{9,10},{10,9},{11,8},{16,18},{17,19... | collective-permute-start | bytes 208904 | tf_op jit(solution)/shard_map/ppermute | solution.py:291
  7.7 0.7 %collective-permute-start.2 = (bf16[16,2176]{1,0:T(8,128)(2,1)S(1)}, bf16[16,2176]{1,0:T(8,128)(2,1)S(1)}, u32[]{:S(2)}, u32[]{:S(2)}) collective-permute-start(bf16[16,2176]{1,0:T(8,128)(2,1)S(1)} %get-tuple-element.21), channel_id=1, source_target_pairs={{0,0},{1,1},{2,2},{3,3},{8,9},{9,8},{10,11},{11,10},{16,16},{17,17... | collective-permute-start | bytes 208904 | tf_op jit(solution)/shard_map/ppermute | solution.py:291
  8.3 2.9 %shard_map.104 = (bf16[1,1,2048,768]{3,2,1,0:T(8,128)(2,1)S(1)}, bf16[1,1,768,2048]{3,2,1,0:T(8,128)(2,1)S(1)}) custom-call(bf16[1,1,2048,768]{3,2,1,0:T(8,128)(2,1)} %up_far.1, bf16[1,1,768,2048]{3,2,1,0:T(8,128)(2,1)} %down_far.1, bf16[16,2176]{1,0:T(8,128)(2,1)S(1)} %get-tuple-element.18.kept._), custom_call_target="tpu_custom_call" | custom-call | bytes 6291456 | tf_op jit(solution)/shard_map/pallas_call | solution.py:272
  11.2 0.6 %collective-permute-done.1.refs_0_ = bf16[16,2176]{1,0:T(8,128)(2,1)S(1)} collective-permute-done((bf16[16,2176]{1,0:T(8,128)(2,1)S(1)}, bf16[16,2176]{1,0:T(8,128)(2,1)S(1)}, u32[]{:S(2)}, u32[]{:S(2)}) %collective-permute-start.1) | collective-permute-done | bytes 69664 | tf_op jit(solution)/shard_map/ppermute | solution.py:291
  11.8 0.0 collective-permute-done.2.refs_1_
  11.8 1.7 %shard_map.105 = (bf16[32,1280]{1,0:T(8,128)(2,1)S(1)}, bf16[32,1280]{1,0:T(8,128)(2,1)S(1)}, bf16[32,1792]{1,0:T(8,128)(2,1)S(1)}, bf16[32,128]{1,0:T(8,128)(2,1)S(1)}) custom-call(bf16[16,2176]{1,0:T(8,128)(2,1)S(1)} %collective-permute-done.1.refs_0_, bf16[16,2176]{1,0:T(8,128)(2,1)S(1)} %collective-permute-done.2.refs_1_, ...), custom_call_target="tpu_custom_call" | custom-call | flops 201326592 | bytes 6291456 | tf_op jit(solution)/shard_map/pallas_call | solution.py:272
  13.5 1.5 %collective-permute-start.8 = (bf16[32,1792]{1,0:T(8,128)(2,1)S(1)}, bf16[32,1792]{1,0:T(8,128)(2,1)S(1)}, u32[]{:S(2)}, u32[]{:S(2)}) collective-permute-start(bf16[32,1792]{1,0:T(8,128)(2,1)S(1)} %get-tuple-element.29), channel_id=1, source_target_pairs={{0,16},{8,24},{16,0},{24,8},{1,17},{9,25},{17,1},{25,9},{2,18},{10... | collective-permute-start | bytes 344072 | tf_op jit(solution)/shard_map/ppermute | solution.py:291
  15.0 3.7 %collective-permute-done.8.refs_2_ = bf16[32,1792]{1,0:T(8,128)(2,1)S(1)} collective-permute-done((bf16[32,1792]{1,0:T(8,128)(2,1)S(1)}, bf16[32,1792]{1,0:T(8,128)(2,1)S(1)}, u32[]{:S(2)}, u32[]{:S(2)}) %collective-permute-start.8) | collective-permute-done | bytes 114720 | tf_op jit(solution)/shard_map/ppermute | solution.py:291
  18.7 0.6 %collective-permute-start.9 = (bf16[32,1792]{1,0:T(8,128)(2,1)S(1)}, bf16[32,1792]{1,0:T(8,128)(2,1)S(1)}, u32[]{:S(2)}, u32[]{:S(2)}) collective-permute-start(bf16[32,1792]{1,0:T(8,128)(2,1)S(1)} %collective-permute-done.8.refs_2_), channel_id=1, source_target_pairs={{0,8},{8,0},{16,24},{24,16},{1,9},{9,1},{17,25},{25,17},{2,10},{10... | collective-permute-start | bytes 344072 | tf_op jit(solution)/shard_map/ppermute | solution.py:291
  19.3 0.0 collective-permute-start.7
  19.4 1.5 %collective-permute-start.3 = (bf16[32,128]{1,0:T(8,128)(2,1)S(1)}, bf16[32,128]{1,0:T(8,128)(2,1)S(1)}, u32[]{:S(2)}, u32[]{:S(2)}) collective-permute-start(bf16[32,128]{1,0:T(8,128)(2,1)S(1)} %get-tuple-element.25.tail_own), channel_id=1, source_target_pairs={{0,4},{4,0},{1,5},{5,1},{2,6},{6,2},{3,7},{7,3},{8,12},{12,8},{9,1... | collective-permute-start | bytes 24584 | tf_op jit(solution)/shard_map/ppermute | solution.py:291
  20.8 1.0 %shard_map.106.body = bf16[32,1024]{1,0:T(8,128)(2,1)S(1)} custom-call(bf16[32,1280]{1,0:T(8,128)(2,1)S(1)} %get-tuple-element.24.own.refs_0_, bf16[1,1,2048,768]{3,2,1,0:T(8,128)(2,1)S(1)} %get-tuple-element.22.refs_2_.up), custom_call_target="tpu_custom_call" | custom-call | flops 100663296 | bytes 3145728 | tf_op jit(solution)/shard_map/pallas_call | solution.py:272
  21.9 1.1 %collective-permute-done.3.tail_other = bf16[32,128]{1,0:T(8,128)(2,1)S(1)} collective-permute-done((bf16[32,128]{1,0:T(8,128)(2,1)S(1)}, bf16[32,128]{1,0:T(8,128)(2,1)S(1)}, u32[]{:S(2)}, u32[]{:S(2)}) %collective-permute-start.3) | collective-permute-done | bytes 8224 | tf_op jit(solution)/shard_map/ppermute | solution.py:291
  23.0 2.8 %collective-permute-start.4 = (bf16[16,1152]{1,0:T(8,128)(2,1)S(1)}, bf16[16,1152]{1,0:T(8,128)(2,1)S(1)}, u32[]{:S(2)}, u32[]{:S(2)}) collective-permute-start(bf16[16,1152]{1,0:T(8,128)(2,1)S(1)} %get-tuple-element.26), channel_id=1, source_target_pairs={{0,6},{1,7},{2,4},{3,5},{4,2},{5,3},{6,0},{7,1},{8,15},{9,14},{10,... | collective-permute-start | bytes 110600 | tf_op jit(solution)/shard_map/ppermute | solution.py:291
  25.8 0.5 %collective-permute-start.5 = (bf16[16,1152]{1,0:T(8,128)(2,1)S(1)}, bf16[16,1152]{1,0:T(8,128)(2,1)S(1)}, u32[]{:S(2)}, u32[]{:S(2)}) collective-permute-start(bf16[16,1152]{1,0:T(8,128)(2,1)S(1)} %get-tuple-element.27), channel_id=1, source_target_pairs={{0,4},{1,5},{2,6},{3,7},{4,0},{5,1},{6,2},{7,3},{8,13},{9,12},{10,... | collective-permute-start | bytes 110600 | tf_op jit(solution)/shard_map/ppermute | solution.py:291
  26.4 2.5 %collective-permute-done.4.high.refs_0_ = bf16[16,1152]{1,0:T(8,128)(2,1)S(1)} collective-permute-done((bf16[16,1152]{1,0:T(8,128)(2,1)S(1)}, bf16[16,1152]{1,0:T(8,128)(2,1)S(1)}, u32[]{:S(2)}, u32[]{:S(2)}) %collective-permute-start.4) | collective-permute-done | bytes 36896 | tf_op jit(solution)/shard_map/ppermute | solution.py:291
  28.8 1.3 %collective-permute-done.5.low.refs_1_ = bf16[16,1152]{1,0:T(8,128)(2,1)S(1)} collective-permute-done((bf16[16,1152]{1,0:T(8,128)(2,1)S(1)}, bf16[16,1152]{1,0:T(8,128)(2,1)S(1)}, u32[]{:S(2)}, u32[]{:S(2)}) %collective-permute-start.5) | collective-permute-done | bytes 36896 | tf_op jit(solution)/shard_map/ppermute | solution.py:291
  30.1 0.0 collective-permute-start.6
  30.1 0.0 collective-permute-done.7.refs_1_
  30.1 0.0 collective-permute-done.9.refs_3_
  30.2 0.6 %shard_map.109 = (bf16[1,1,512,768]{3,2,1,0:T(8,128)(2,1)S(1)}, bf16[1,1,768,512]{3,2,1,0:T(8,128)(2,1)S(1)}) custom-call(bf16[32,1280]{1,0:T(8,128)(2,1)S(1)} %get-tuple-element.24.own.refs_0_, bf16[32,1280]{1,0:T(8,128)(2,1)S(1)} %collective-permute-done.7.refs_1_, bf16[32,1792]{1,0:T(8,128)(2,1)S(1)} %collective-permute-done.8.refs_2_, ...), custom_call_target="tpu_custom_call" | custom-call | flops 201326592 | bytes 1572864 | tf_op jit(solution)/shard_map/pallas_call | solution.py:272
  30.8 0.6 %collective-permute-done.6.refs_2_ = bf16[16,1152]{1,0:T(8,128)(2,1)S(1)} collective-permute-done((bf16[16,1152]{1,0:T(8,128)(2,1)S(1)}, bf16[16,1152]{1,0:T(8,128)(2,1)S(1)}, u32[]{:S(2)}, u32[]{:S(2)}) %collective-permute-start.6) | collective-permute-done | bytes 36896 | tf_op jit(solution)/shard_map/ppermute | solution.py:291
  31.3 1.4 %shard_map.110 = (bf16[1,128,2048]{2,1,0:T(8,128)(2,1)}, bf16[1,1,4,4]{3,2,1,0:T(4,128)(2,1)}, bf16[1,1,512,768]{3,2,1,0:T(8,128)(2,1)}, bf16[1,1,768,512]{3,2,1,0:T(8,128)(2,1)}) custom-call(bf16[16,1152]{1,0:T(8,128)(2,1)S(1)} %collective-permute-done.4.high.refs_0_, bf16[16,1152]{1,0:T(8,128)(2,1)S(1)} %collective-permute-done.5.low.refs_1_, ...), custom_call_target="tpu_custom_call" | custom-call | flops 16777216 | bytes 524288 | tf_op jit(solution)/shard_map/pallas_call | solution.py:272
  (3 shorter events, 0.0 us)
Async XLA Ops:
  2.2 1.5 %collective-permute-start = (bf16[16,2176]{1,0:T(8,128)(2,1)S(1)}, bf16[16,2176]{1,0:T(8,128)(2,1)S(1)}, u32[]{:S(2)}, u32[]{:S(2)}) collective-permute-start(bf16[16,2176]{1,0:T(8,128)(2,1)S(1)} %get-tuple-element.19), channel_id=1, source_target_pairs={{0,8},{8,0},{16,24},{24,16},{1,9},{9,1},{17,25},{25,17},{2,10},{10... | collective-permute-start | bytes 208904 | tf_op jit(solution)/shard_map/ppermute | solution.py:291
  3.7 8.1 %collective-permute-start.1 = (bf16[16,2176]{1,0:T(8,128)(2,1)S(1)}, bf16[16,2176]{1,0:T(8,128)(2,1)S(1)}, u32[]{:S(2)}, u32[]{:S(2)}) collective-permute-start(bf16[16,2176]{1,0:T(8,128)(2,1)S(1)} %get-tuple-element.20), channel_id=1, source_target_pairs={{0,2},{1,3},{2,0},{3,1},{8,11},{9,10},{10,9},{11,8},{16,18},{17,19... | collective-permute-start | bytes 208904 | tf_op jit(solution)/shard_map/ppermute | solution.py:291
  7.7 4.2 %collective-permute-start.2 = (bf16[16,2176]{1,0:T(8,128)(2,1)S(1)}, bf16[16,2176]{1,0:T(8,128)(2,1)S(1)}, u32[]{:S(2)}, u32[]{:S(2)}) collective-permute-start(bf16[16,2176]{1,0:T(8,128)(2,1)S(1)} %get-tuple-element.21), channel_id=1, source_target_pairs={{0,0},{1,1},{2,2},{3,3},{8,9},{9,8},{10,11},{11,10},{16,16},{17,17... | collective-permute-start | bytes 208904 | tf_op jit(solution)/shard_map/ppermute | solution.py:291
  13.5 5.2 %collective-permute-start.8 = (bf16[32,1792]{1,0:T(8,128)(2,1)S(1)}, bf16[32,1792]{1,0:T(8,128)(2,1)S(1)}, u32[]{:S(2)}, u32[]{:S(2)}) collective-permute-start(bf16[32,1792]{1,0:T(8,128)(2,1)S(1)} %get-tuple-element.29), channel_id=1, source_target_pairs={{0,16},{8,24},{16,0},{24,8},{1,17},{9,25},{17,1},{25,9},{2,18},{10... | collective-permute-start | bytes 344072 | tf_op jit(solution)/shard_map/ppermute | solution.py:291
  18.7 11.4 %collective-permute-start.9 = (bf16[32,1792]{1,0:T(8,128)(2,1)S(1)}, bf16[32,1792]{1,0:T(8,128)(2,1)S(1)}, u32[]{:S(2)}, u32[]{:S(2)}) collective-permute-start(bf16[32,1792]{1,0:T(8,128)(2,1)S(1)} %collective-permute-done.8.refs_2_), channel_id=1, source_target_pairs={{0,8},{8,0},{16,24},{24,16},{1,9},{9,1},{17,25},{25,17},{2,10},{10... | collective-permute-start | bytes 344072 | tf_op jit(solution)/shard_map/ppermute | solution.py:291
  19.3 10.8 %collective-permute-start.7 = (bf16[32,1280]{1,0:T(8,128)(2,1)S(1)}, bf16[32,1280]{1,0:T(8,128)(2,1)S(1)}, u32[]{:S(2)}, u32[]{:S(2)}) collective-permute-start(bf16[32,1280]{1,0:T(8,128)(2,1)S(1)} %get-tuple-element.28), channel_id=1, source_target_pairs={{0,8},{8,0},{16,24},{24,16},{1,9},{9,1},{17,25},{25,17},{2,10},{10... | collective-permute-start | bytes 245768 | tf_op jit(solution)/shard_map/ppermute | solution.py:291
  19.4 3.7 %collective-permute-start.3 = (bf16[32,128]{1,0:T(8,128)(2,1)S(1)}, bf16[32,128]{1,0:T(8,128)(2,1)S(1)}, u32[]{:S(2)}, u32[]{:S(2)}) collective-permute-start(bf16[32,128]{1,0:T(8,128)(2,1)S(1)} %get-tuple-element.25.tail_own), channel_id=1, source_target_pairs={{0,4},{4,0},{1,5},{5,1},{2,6},{6,2},{3,7},{7,3},{8,12},{12,8},{9,1... | collective-permute-start | bytes 24584 | tf_op jit(solution)/shard_map/ppermute | solution.py:291
  23.0 5.8 %collective-permute-start.4 = (bf16[16,1152]{1,0:T(8,128)(2,1)S(1)}, bf16[16,1152]{1,0:T(8,128)(2,1)S(1)}, u32[]{:S(2)}, u32[]{:S(2)}) collective-permute-start(bf16[16,1152]{1,0:T(8,128)(2,1)S(1)} %get-tuple-element.26), channel_id=1, source_target_pairs={{0,6},{1,7},{2,4},{3,5},{4,2},{5,3},{6,0},{7,1},{8,15},{9,14},{10,... | collective-permute-start | bytes 110600 | tf_op jit(solution)/shard_map/ppermute | solution.py:291
  25.8 4.3 %collective-permute-start.5 = (bf16[16,1152]{1,0:T(8,128)(2,1)S(1)}, bf16[16,1152]{1,0:T(8,128)(2,1)S(1)}, u32[]{:S(2)}, u32[]{:S(2)}) collective-permute-start(bf16[16,1152]{1,0:T(8,128)(2,1)S(1)} %get-tuple-element.27), channel_id=1, source_target_pairs={{0,4},{1,5},{2,6},{3,7},{4,0},{5,1},{6,2},{7,3},{8,13},{9,12},{10,... | collective-permute-start | bytes 110600 | tf_op jit(solution)/shard_map/ppermute | solution.py:291
  30.1 1.2 %collective-permute-start.6 = (bf16[16,1152]{1,0:T(8,128)(2,1)S(1)}, bf16[16,1152]{1,0:T(8,128)(2,1)S(1)}, u32[]{:S(2)}, u32[]{:S(2)}) collective-permute-start(bf16[16,1152]{1,0:T(8,128)(2,1)S(1)} %shard_map.108), channel_id=1, source_target_pairs={{0,8},{8,0},{16,24},{24,16},{1,9},{9,1},{17,25},{25,17},{2,10},{10... | collective-permute-start | bytes 110600 | tf_op jit(solution)/shard_map/ppermute | solution.py:291

commit v3 on v2

v3 whole, which is shorter than its diff:
```python
import functools
import itertools

import jax
import jax.numpy as jnp
from jax import lax
from jax.experimental import pallas as pl
from jax.experimental.pallas import tpu as pltpu
from jax.sharding import PartitionSpec as P


BF16 = jnp.bfloat16
F32 = jnp.float32
LANES = 128
KERNEL_VMEM = 24 << 20
PIECES = 1


def row_marks(rows, width, capacity):
    row = lax.broadcasted_iota(jnp.int32, (rows, width), 0)
    return lax.shift_right_logical(row, capacity.bit_length() - 1), row & (capacity - 1)


def stacked(refs, columns=slice(None)):
    return jnp.concatenate([ref[:, columns].astype(F32) for ref in refs], axis=0)


def upper_rows(value):
    row = lax.broadcasted_iota(jnp.int32, value.shape, 0)
    return row < value.shape[0] // 2


def turned(value):
    return pltpu.roll(value, value.shape[0] // 2, 0)


def in_pairs(experts, replicas):
    return experts == 4 and replicas == 4


FIRST_SLOT = (2, 1)
SECOND_SLOT = (0, 3)


def partner_of(group, second_first):
    side = (lax.axis_index("dp") & 1) ^ lax.shift_right_logical(group, 1)
    second = 1 - (group & 1) if second_first else group & 1
    in_first = FIRST_SLOT[0] + side * (FIRST_SLOT[1] - FIRST_SLOT[0])
    in_second = SECOND_SLOT[0] + side * (SECOND_SLOT[1] - SECOND_SLOT[0])
    return in_first + second * (in_second - in_first)


def pack_kernel(acts_far, grads_far, ids_far, counts_far, probs_far, *refs):
    outs, acts, grads, ids, counts, probs, sems = refs[:-6], *refs[-6:]
    tokens, width = acts.shape[1:]
    spans = [pl.ds(k * width // PIECES, width // PIECES) for k in range(PIECES)]
    pairs = [(ids_far, ids), (counts_far, counts), (probs_far, probs)]
    for span in spans:
        pairs.append((acts_far.at[:, :, span], acts.at[:, :, span]))
        pairs.append((grads_far.at[:, :, span], grads.at[:, :, span]))
    copies = [pltpu.make_async_copy(a, b, sems.at[k]) for k, (a, b) in enumerate(pairs)]
    for copy in copies:
        copy.start()
    for copy in copies[:3]:
        copy.wait()
    experts, capacity = ids.shape[2:]
    rows = experts * capacity
    paired = in_pairs(experts, lax.axis_size("dp"))

    def dest_of(group):
        return partner_of(group, True) ^ lax.axis_index("expert") if paired else group

    group, slot = row_marks(rows, capacity, capacity)
    dest = dest_of(group)
    id_rows = ids[0, 0].astype(F32)
    prob_rows = probs[0, 0].astype(F32)
    id_grid = jnp.zeros((rows, capacity), F32)
    prob_grid = jnp.zeros((rows, capacity), F32)
    for e in range(experts):
        here = dest == e
        id_grid = jnp.where(here, id_rows[e : e + 1], id_grid)
        prob_grid = jnp.where(here, prob_rows[e : e + 1], prob_grid)
    at_slot = lax.broadcasted_iota(jnp.int32, (rows, capacity), 1) == slot
    id_col = jnp.sum(jnp.where(at_slot, id_grid, 0.0), axis=1, keepdims=True)
    prob_col = jnp.sum(jnp.where(at_slot, prob_grid, 0.0), axis=1, keepdims=True)
    dest_wide = dest_of(row_marks(rows, experts, capacity)[0])
    at_dest = lax.broadcasted_iota(jnp.int32, (rows, experts), 1) == dest_wide
    count_row = counts[0].astype(F32)
    count_col = jnp.sum(jnp.where(at_dest, count_row, 0.0), axis=1, keepdims=True)
    live = slot[:, :1].astype(F32) < count_col
    prob_col = jnp.where(live, prob_col, 0.0)
    lane = lax.broadcasted_iota(jnp.int32, (rows, tokens), 1).astype(F32)
    hit = jnp.where(lane == id_col, 1.0, 0.0)
    pick_act = hit.astype(BF16)
    pick_grad = jnp.where(live, hit, 0.0).astype(BF16)
    tail_lane = lax.broadcasted_iota(jnp.int32, (rows, LANES), 1)
    tail = jnp.where(tail_lane == 0, prob_col, jnp.where(tail_lane == 1, id_col, 0.0))
    size = rows // len(outs)

    def put(value, columns):
        for k, out in enumerate(outs):
            out[:, columns] = value[k * size : (k + 1) * size].astype(BF16)

    put(tail, pl.ds(2 * width, LANES))
    for piece in range(PIECES):
        step = width // PIECES
        copies[3 + 2 * piece].wait()
        picked = jnp.dot(pick_act, acts[0, :, spans[piece]], preferred_element_type=F32)
        put(picked, pl.ds(piece * step, step))
        copies[4 + 2 * piece].wait()
        picked = jnp.dot(pick_grad, grads[0, :, spans[piece]], preferred_element_type=F32)
        put(picked, pl.ds(width + piece * step, step))


def join_kernel(kept, came, first, second):
    mine, other = kept[...].astype(F32), came[...].astype(F32)
    upper = upper_rows(mine)
    first[...] = jnp.where(upper, turned(mine), other).astype(BF16)
    second[...] = jnp.where(upper, mine, turned(other)).astype(BF16)


def other_kernel(first, second, out):
    value = first[...].astype(F32)
    out[...] = jnp.where(upper_rows(value), turned(value), second[...].astype(F32)).astype(BF16)


def expert_kernel(replicas, n_blocks, *refs):
    blocks = refs[:n_blocks]
    up, down = refs[n_blocks : n_blocks + 2]
    outs = refs[n_blocks + 2 : -2]
    tail_out, scaled = refs[-2:]
    hidden_width, width = down.shape[2:]
    rows = sum(block.shape[0] for block in blocks)
    part = width // replicas
    act_rows = stacked(blocks, slice(0, width)).astype(BF16)
    pre_act = jnp.dot(act_rows, up[0, 0], preferred_element_type=F32)
    grad_rows = stacked(blocks, slice(width, 2 * width))
    tail = stacked(blocks, slice(2 * width, 2 * width + LANES))
    prob = tail[:, 0:1]
    grad_proj = lax.dot_general(
        grad_rows.astype(BF16), down[0, 0], (((1,), (1,)), ((), ())), preferred_element_type=F32
    )
    scaled[:rows] = act_rows
    scaled[rows:] = (prob * grad_rows).astype(BF16)
    logistic = jax.nn.sigmoid(pre_act)
    hidden = (pre_act * logistic).astype(BF16).astype(F32)
    slope = logistic * (1.0 + pre_act * (1.0 - logistic))
    act_grad = prob * grad_proj * slope
    gate = jnp.sum(hidden * grad_proj, axis=1, keepdims=True)
    lane = lax.broadcasted_iota(jnp.int32, (rows, LANES), 1)
    tail_out[...] = jnp.where(lane == 0, gate, tail).astype(BF16)
    both = jnp.concatenate([act_grad, hidden], axis=0).astype(BF16)
    place = lax.axis_index("dp") if replicas == 4 else 0
    for k, out in enumerate(outs if len(outs) > 1 else [outs[0].at[k] for k in range(replicas)]):
        wide = out.shape[1] - hidden_width
        column = pl.multiple_of((place ^ k) // (wide // part) * wide, LANES)
        out[:, :hidden_width] = both
        out[:, hidden_width:] = scaled[:, pl.ds(column, wide)]


def back_kernel(own, up, body):
    rows, hidden_width = body.shape[0], up.shape[3]
    body[...] = lax.dot_general(
        own[:rows, :hidden_width], up[0, 0], (((1,), (1,)), ((), ())), preferred_element_type=F32
    ).astype(BF16)


def reply_kernel(body, tail_own, tail_other, *outs):
    rows, width = body.shape
    lane = lax.broadcasted_iota(jnp.int32, (rows, LANES), 1)
    tail = jnp.where(lane == 0, tail_other[...].astype(F32), tail_own[...].astype(F32))
    values = body[...].astype(F32)
    size = rows // len(outs)
    for k, out in enumerate(outs):
        out[:, :width] = values[k * size : (k + 1) * size].astype(BF16)
        out[:, width:] = tail[k * size : (k + 1) * size].astype(BF16)


def weight_kernel(rows, n_blocks, *refs):
    blocks = refs[:n_blocks]
    if n_blocks == 1:
        blocks = [blocks[0].at[k] for k in range(blocks[0].shape[0])]
    grad_up, grad_down = refs[n_blocks:]

    def first_of(value):
        row = lax.broadcasted_iota(jnp.int32, value.shape, 0)
        return (row & (2 * rows - 1)) < rows

    hidden_width = grad_up.shape[3]
    part = grad_up.shape[2]
    both = jnp.concatenate([block[:, :hidden_width] for block in blocks], axis=0)
    columns = []
    for block in blocks:
        if block.shape[1] > hidden_width + part:
            begin = hidden_width + (lax.axis_index("dp") & 1) * part
            columns.append(block[:, pl.ds(pl.multiple_of(begin, LANES), part)])
        else:
            columns.append(block[:, hidden_width:])
    sides = jnp.concatenate(columns, axis=0)
    act_grad = jnp.where(first_of(both), both, jnp.zeros_like(both))
    grad_up[0, 0] = lax.dot_general(
        sides, act_grad, (((0,), (0,)), ((), ())), preferred_element_type=F32
    ).astype(BF16)
    scaled = jnp.where(first_of(sides), jnp.zeros_like(sides), sides)
    grad_down[0, 0] = lax.dot_general(
        both, scaled, (((0,), (0,)), ((), ())), preferred_element_type=F32
    ).astype(BF16)


def combine_kernel(capacity, sections, n_blocks, *refs):
    blocks = refs[:n_blocks]
    up_near, down_near, prev_far, gate_far, up_far, down_far, prev, gate, sems = refs[n_blocks:]
    tokens, width = prev.shape[1:]
    experts = gate.shape[2]
    paired = in_pairs(experts, lax.axis_size("dp"))
    half = width // 2
    rows = capacity * experts
    spans = [pl.ds(k * half, half) for k in range(2)]
    pairs = [(prev.at[:, :, span], prev_far.at[:, :, span]) for span in spans]
    pairs += [(gate, gate_far), (up_near, up_far), (down_near, down_far)]
    copies = [pltpu.make_async_copy(a, b, sems.at[k]) for k, (a, b) in enumerate(pairs)]
    copies[3].start()
    copies[4].start()
    if paired:
        first, second, came = [block[...].astype(F32) for block in blocks]
        mine = jnp.where(upper_rows(first), first, turned(second))
        joined = jnp.concatenate([mine, came], axis=0)
    else:
        joined = stacked(blocks)
    body, tail = joined[:, :width].astype(BF16), joined[:, width:]
    lane = lax.broadcasted_iota(jnp.int32, (rows, tokens), 1).astype(F32)
    kept = jnp.where(lax.axis_index("pipe") == sections - 1, 0.0, 1.0)
    one_hot = jnp.where(lane == tail[:, 1:2], kept, 0.0).astype(BF16)
    for part, span in enumerate(spans):
        prev[0, :, span] = lax.dot_general(
            one_hot,
            body[:, part * half : (part + 1) * half],
            (((0,), (0,)), ((), ())),
            preferred_element_type=F32,
        ).astype(BF16)
        copies[part].start()
    _, slot = row_marks(rows, capacity, capacity)
    at_slot = lax.broadcasted_iota(jnp.int32, (rows, capacity), 1) == slot
    gates = jnp.where(at_slot, tail[:, 0:1], 0.0).astype(BF16)
    column = lax.broadcasted_iota(jnp.int32, (experts, rows), 1)
    source = lax.shift_right_logical(column, capacity.bit_length() - 1)
    if paired:
        source = partner_of(source, False) ^ lax.axis_index("expert")
    wanted = source == lax.broadcasted_iota(jnp.int32, (experts, rows), 0)
    gate[0, 0] = jnp.dot(
        jnp.where(wanted, 1.0, 0.0).astype(BF16), gates, preferred_element_type=F32
    ).astype(BF16)
    copies[2].start()
    for copy in copies:
        copy.wait()


def call(kernel, out_shape, args, flops, n_bytes, scratch=(), far=(), far_out=False):
    near_spec = pl.BlockSpec(memory_space=pltpu.VMEM)
    far_spec = pl.BlockSpec(memory_space=pl.ANY)
    args = [
        pltpu.with_memory_space_constraint(a, pltpu.HBM if k in far else pltpu.VMEM)
        for k, a in enumerate(args)
    ]
    if not far_out:
        out_shape = [pltpu.VMEM(s.shape, s.dtype) for s in out_shape]
    return pl.pallas_call(
        kernel,
        out_shape=out_shape,
        in_specs=[far_spec if k in far else near_spec for k in range(len(args))],
        out_specs=[far_spec if far_out else near_spec] * len(out_shape),
        scratch_shapes=list(scratch),
        compiler_params=pltpu.CompilerParams(vmem_limit_bytes=KERNEL_VMEM),
        cost_estimate=pl.CostEstimate(flops=flops, bytes_accessed=n_bytes, transcendentals=0),
    )(*args)


def permuted(block, axes, route):
    sizes = [lax.axis_size(axis) for axis in axes]

    def flat(place):
        return functools.reduce(lambda total, pair: total * pair[1] + pair[0], zip(place, sizes), 0)

    places = list(itertools.product(*[range(size) for size in sizes]))
    pairs = [(flat(place), flat(route(place))) for place in places]
    return lax.ppermute(block, axes if len(axes) > 1 else axes[0], pairs)


def message_shapes(paired, rows, width, dtype=BF16):
    if paired:
        return [jax.ShapeDtypeStruct((rows // 2, width), dtype)] * 2
    return [jax.ShapeDtypeStruct((rows, width), dtype)]


def traded(block, axis):
    return lax.all_to_all(block, axis, split_axis=0, concat_axis=0, tiled=True)


def swapped(block):
    return permuted(block, ("dp",), lambda p: (p[0] ^ 1,))


def share_shapes(replicas, rows, hidden_width, part):
    if replicas != 4:
        return [jax.ShapeDtypeStruct((replicas, rows, hidden_width + part), BF16)]
    widths = (hidden_width + part, hidden_width + part, hidden_width + 2 * part)
    return [jax.ShapeDtypeStruct((rows, width), BF16) for width in widths]


def shared(blocks, replicas):
    if replicas != 4:
        return [traded(blocks[0], "dp")]
    own, near, far = blocks
    crossed = permuted(far, ("dp",), lambda p: (p[0] ^ 2,))
    beside = swapped(near)
    passed = swapped(crossed)
    return [own, beside, crossed, passed]


def per_device(activations, out_grad, slot_token, slot_count, gate_prob, w_up, w_down):
    tokens, width = activations.shape[1:]
    experts, capacity = slot_token.shape[2:]
    hidden_width = w_up.shape[3]
    replicas = lax.axis_size("dp")
    sections = lax.axis_size("pipe")
    rows = capacity * experts
    part = width // replicas
    paired = in_pairs(experts, replicas)
    sources = (activations, out_grad, slot_token, slot_count, gate_prob)
    packed = call(
        pack_kernel,
        message_shapes(paired, rows, 2 * width + LANES),
        sources,
        4 * rows * tokens * width,
        4 * tokens * width,
        [pltpu.VMEM(a.shape, a.dtype) for a in sources] + [pltpu.SemaphoreType.DMA((3 + 2 * PIECES,))],
        far=range(5),
    )
    if paired:
        kept, sent = packed
        first, second = call(
            join_kernel,
            message_shapes(paired, rows, 2 * width + LANES),
            (kept, swapped(sent)),
            20_000_000_000,
            4 * rows * width,
        )
        across = ("dp", "expert")

        def first_slot(p):
            return (p[0], p[1] ^ FIRST_SLOT[p[0] & 1])

        def second_slot(p):
            return (p[0], p[1] ^ SECOND_SLOT[p[0] & 1])

        held = [permuted(first, across, first_slot), permuted(second, across, second_slot)]
    else:
        held = [traded(packed[0], "expert")]
    made = call(
        functools.partial(expert_kernel, replicas, len(held)),
        share_shapes(replicas, 2 * rows, hidden_width, part)
        + [jax.ShapeDtypeStruct((rows, LANES), BF16)],
        (*held, w_up, w_down),
        4 * rows * width * hidden_width,
        4 * width * hidden_width,
        [pltpu.VMEM((2 * rows, width), BF16)],
    )
    shares, tail_own = made[:-1], made[-1]
    joined = shared(shares, replicas)
    own = shares[0] if len(shares) > 1 else shares[0][0]
    tail_other = permuted(tail_own, ("pipe",), lambda p: ((p[0] + 1) % sections,))
    (body,) = call(
        back_kernel,
        [jax.ShapeDtypeStruct((rows, width), BF16)],
        (own, w_up),
        2 * rows * width * hidden_width,
        2 * width * hidden_width,
    )
    replies = call(
        reply_kernel,
        message_shapes(paired, rows, width + LANES),
        (body, tail_own, tail_other),
        0,
        4 * rows * width,
    )
    if paired:
        every = ("dp", "pipe", "expert")

        def before(p, slot):
            return (p[0], (p[1] - 1) % sections, p[2] ^ slot[p[0] & 1])

        high = permuted(replies[0], every, lambda p: before(p, FIRST_SLOT))
        low = permuted(replies[1], every, lambda p: before(p, SECOND_SLOT))
        (other,) = call(
            other_kernel,
            [jax.ShapeDtypeStruct((rows // 2, width + LANES), BF16)],
            (high, low),
            0,
            4 * rows * width,
        )
        returned = [high, low, swapped(other)]
    else:
        moved = permuted(replies[0], ("pipe",), lambda p: ((p[0] - 1) % sections,))
        returned = [traded(moved, "expert")]
    weight_grads = [
        jax.ShapeDtypeStruct((1, 1, part, hidden_width), BF16),
        jax.ShapeDtypeStruct((1, 1, hidden_width, part), BF16),
    ]
    near_grads = call(
        functools.partial(weight_kernel, rows, len(joined)),
        weight_grads,
        tuple(joined),
        4 * replicas * rows * part * hidden_width,
        4 * part * hidden_width,
    )
    token_grads = [
        jax.ShapeDtypeStruct((1, tokens, width), BF16),
        jax.ShapeDtypeStruct((1, 1, experts, capacity), BF16),
    ]
    grad_prev, grad_gate, grad_up, grad_down = call(
        functools.partial(combine_kernel, capacity, sections, len(returned)),
        token_grads + weight_grads,
        (*returned, *near_grads),
        2 * rows * tokens * width,
        2 * tokens * width,
        [pltpu.VMEM(s.shape, s.dtype) for s in token_grads] + [pltpu.SemaphoreType.DMA((5,))],
        far_out=True,
    )
    return grad_prev, grad_gate, grad_up, grad_down


def solution(mesh):
    by_token = ("dp", "expert")
    placed = (
        P("pipe", by_token, None),
        P("pipe", by_token, None),
        P("pipe", by_token, None, None),
        P("pipe", by_token, None),
        P("pipe", by_token, None, None),
        P("pipe", "expert", None, None),
        P("pipe", "expert", None, None),
    )
    return jax.shard_map(
        per_device,
        mesh=mesh,
        in_specs=placed,
        out_specs=(
            P("pipe", by_token, None),
            P("pipe", by_token, None, None),
            P("pipe", "expert", "dp", None),
            P("pipe", "expert", None, "dp"),
        ),
        check_vma=False,
    )
```

time: 32.9 us -> 32 us (0.973)
  Pallas kernels: 9.1 us -> 5.84 us
  starting transfers between devices: 12.2 us -> 14.6 us
    pallas_call x9 -> x8, Pallas kernels: 9.1 us -> 5.84 us  [call(): pl.pallas_call(kernel, out_shape=out_shape, in_specs=[far_spec if k in fa...]
    ppermute x10, starting transfers between devices: 12.2 us -> 14.6 us  [permuted(): return lax.ppermute(block, axes if len(axes) > 1 else axes[0], pairs)]
  transfers between devices with their start and end apart: 10 -> 10, of which waited for: 7 -> 7; matrix products, arithmetic and copies ran while one was open for 0% -> 0% of each run, Pallas kernels for 14% -> 5%
where the time goes in v3:
time: 32 us; the launch traced here: 31.8 us
  starting transfers between devices  14.6 us (46%)
  waiting for transfers between devices  10.6 us (33%)
  Pallas kernels  5.84 us (18%)
  between operations  0.7 us (2%)
    ppermute x10, starting transfers between devices, permuted(): return lax.ppermute(block, axes if len(axes) > 1 else axes[0], pairs)  14.6 us
    ppermute x10, waiting for transfers between devices, permuted(): return lax.ppermute(block, axes if len(axes) > 1 else axes[0], pairs)  10.6 us
    pallas_call x8, Pallas kernels, call(): pl.pallas_call(kernel, out_shape=out_shape, in_specs=[far_spec if k in fa...  5.84 us
  transfers between devices with their start and end apart: 10, of which 7 were waited for; matrix products, arithmetic and copies ran while one was open for 0% of the time, Pallas kernels for 5%

profile of v3, /device:TPU:0, one launch (start us, length us, event | category | flops | bytes accessed | tf_op | source)
XLA Modules:
  0.0 31.8 jit_solution(13833568118991512249)
XLA Ops:
  0.6 1.5 %shard_map.102 = (bf16[8,4224]{1,0:T(8,128)(2,1)S(1)}, bf16[8,4224]{1,0:T(8,128)(2,1)S(1)}) custom-call(bf16[1,128,2048]{2,1,0:T(8,128)(2,1)} %acts_far.1, bf16[1,128,2048]{2,1,0:T(8,128)(2,1)} %grads_far.1, s32[1,1,4,4]{3,2,1,0:T(4,128)} %ids_far.1, s32[1,1,4]{2,1,0:T(1,128)} %counts_far.1, bf16[1,1,4,4]{3,2,1,0:T(4,128)(2,1)} %probs_far.1), custom_call_target="tpu_custom_call" | custom-call | flops 16777216 | bytes 1048576 | tf_op jit(solution)/shard_map/pallas_call | solution.py:267
  2.1 0.6 %collective-permute-start = (bf16[8,4224]{1,0:T(8,128)(2,1)S(1)}, bf16[8,4224]{1,0:T(8,128)(2,1)S(1)}, u32[]{:S(2)}, u32[]{:S(2)}) collective-permute-start(bf16[8,4224]{1,0:T(8,128)(2,1)S(1)} %get-tuple-element.17), channel_id=1, source_target_pairs={{0,8},{8,0},{16,24},{24,16},{1,9},{9,1},{17,25},{25,17},{2,10},{10... | collective-permute-start | bytes 202760 | tf_op jit(solution)/shard_map/ppermute | solution.py:286
  2.7 0.9 %collective-permute-done.came = bf16[8,4224]{1,0:T(8,128)(2,1)S(1)} collective-permute-done((bf16[8,4224]{1,0:T(8,128)(2,1)S(1)}, bf16[8,4224]{1,0:T(8,128)(2,1)S(1)}, u32[]{:S(2)}, u32[]{:S(2)}) %collective-permute-start) | collective-permute-done | bytes 67616 | tf_op jit(solution)/shard_map/ppermute | solution.py:286
  3.6 0.0 copy-start
  3.6 0.0 copy-start.1
  3.7 4.0 %collective-permute-start.1 = (bf16[8,4224]{1,0:T(8,128)(2,1)S(1)}, bf16[8,4224]{1,0:T(8,128)(2,1)S(1)}, u32[]{:S(2)}, u32[]{:S(2)}) collective-permute-start(bf16[8,4224]{1,0:T(8,128)(2,1)S(1)} %get-tuple-element.18), channel_id=1, source_target_pairs={{0,2},{1,3},{2,0},{3,1},{8,9},{9,8},{10,11},{11,10},{16,18},{17,19... | collective-permute-start | bytes 202760 | tf_op jit(solution)/shard_map/ppermute | solution.py:286
  7.6 0.7 %collective-permute-start.2 = (bf16[8,4224]{1,0:T(8,128)(2,1)S(1)}, bf16[8,4224]{1,0:T(8,128)(2,1)S(1)}, u32[]{:S(2)}, u32[]{:S(2)}) collective-permute-start(bf16[8,4224]{1,0:T(8,128)(2,1)S(1)} %get-tuple-element.19), channel_id=1, source_target_pairs={{0,0},{1,1},{2,2},{3,3},{8,11},{9,10},{10,9},{11,8},{16,16},{17,17... | collective-permute-start | bytes 202760 | tf_op jit(solution)/shard_map/ppermute | solution.py:286
  8.3 1.6 %collective-permute-done.1.refs_0_ = bf16[8,4224]{1,0:T(8,128)(2,1)S(1)} collective-permute-done((bf16[8,4224]{1,0:T(8,128)(2,1)S(1)}, bf16[8,4224]{1,0:T(8,128)(2,1)S(1)}, u32[]{:S(2)}, u32[]{:S(2)}) %collective-permute-start.1) | collective-permute-done | bytes 67616 | tf_op jit(solution)/shard_map/ppermute | solution.py:286
  9.9 0.0 collective-permute-done.2.refs_1_
  9.9 0.0 copy-done
  9.9 0.0 copy-done.1
  9.9 1.4 %shard_map.104 = (bf16[32,1280]{1,0:T(8,128)(2,1)S(1)}, bf16[32,1280]{1,0:T(8,128)(2,1)S(1)}, bf16[32,1792]{1,0:T(8,128)(2,1)S(1)}, bf16[16,128]{1,0:T(8,128)(2,1)S(1)}) custom-call(bf16[8,4224]{1,0:T(8,128)(2,1)S(1)} %collective-permute-done.1.refs_0_, bf16[8,4224]{1,0:T(8,128)(2,1)S(1)} %collective-permute-done.2.refs_1_, ...), custom_call_target="tpu_custom_call" | custom-call | flops 100663296 | bytes 6291456 | tf_op jit(solution)/shard_map/pallas_call | solution.py:267
  11.3 1.9 %collective-permute-start.8 = (bf16[32,1792]{1,0:T(8,128)(2,1)S(1)}, bf16[32,1792]{1,0:T(8,128)(2,1)S(1)}, u32[]{:S(2)}, u32[]{:S(2)}) collective-permute-start(bf16[32,1792]{1,0:T(8,128)(2,1)S(1)} %get-tuple-element.25), channel_id=1, source_target_pairs={{0,16},{8,24},{16,0},{24,8},{1,17},{9,25},{17,1},{25,9},{2,18},{10... | collective-permute-start | bytes 344072 | tf_op jit(solution)/shard_map/ppermute | solution.py:286
  13.2 2.9 %collective-permute-done.8.refs_2_ = bf16[32,1792]{1,0:T(8,128)(2,1)S(1)} collective-permute-done((bf16[32,1792]{1,0:T(8,128)(2,1)S(1)}, bf16[32,1792]{1,0:T(8,128)(2,1)S(1)}, u32[]{:S(2)}, u32[]{:S(2)}) %collective-permute-start.8) | collective-permute-done | bytes 114720 | tf_op jit(solution)/shard_map/ppermute | solution.py:286
  16.1 2.3 %collective-permute-start.9 = (bf16[32,1792]{1,0:T(8,128)(2,1)S(1)}, bf16[32,1792]{1,0:T(8,128)(2,1)S(1)}, u32[]{:S(2)}, u32[]{:S(2)}) collective-permute-start(bf16[32,1792]{1,0:T(8,128)(2,1)S(1)} %collective-permute-done.8.refs_2_), channel_id=1, source_target_pairs={{0,8},{8,0},{16,24},{24,16},{1,9},{9,1},{17,25},{25,17},{2,10},{10... | collective-permute-start | bytes 344072 | tf_op jit(solution)/shard_map/ppermute | solution.py:286
  18.4 0.0 collective-permute-start.7
  18.4 1.6 %collective-permute-start.3 = (bf16[16,128]{1,0:T(8,128)(2,1)S(1)}, bf16[16,128]{1,0:T(8,128)(2,1)S(1)}, u32[]{:S(2)}, u32[]{:S(2)}) collective-permute-start(bf16[16,128]{1,0:T(8,128)(2,1)S(1)} %get-tuple-element.21.tail_own), channel_id=1, source_target_pairs={{0,4},{4,0},{1,5},{5,1},{2,6},{6,2},{3,7},{7,3},{8,12},{12,8},{9,1... | collective-permute-start | bytes 12296 | tf_op jit(solution)/shard_map/ppermute | solution.py:286
  20.0 0.9 %shard_map.105.body = bf16[16,2048]{1,0:T(8,128)(2,1)S(1)} custom-call(bf16[32,1280]{1,0:T(8,128)(2,1)S(1)} %get-tuple-element.20.own.refs_0_, bf16[1,1,2048,768]{3,2,1,0:T(8,128)(2,1)S(1)} %copy-done), custom_call_target="tpu_custom_call" | custom-call | flops 50331648 | bytes 3145728 | tf_op jit(solution)/shard_map/pallas_call | solution.py:267
  20.9 1.1 %collective-permute-done.3.tail_other = bf16[16,128]{1,0:T(8,128)(2,1)S(1)} collective-permute-done((bf16[16,128]{1,0:T(8,128)(2,1)S(1)}, bf16[16,128]{1,0:T(8,128)(2,1)S(1)}, u32[]{:S(2)}, u32[]{:S(2)}) %collective-permute-start.3) | collective-permute-done | bytes 4128 | tf_op jit(solution)/shard_map/ppermute | solution.py:286
  22.0 3.1 %collective-permute-start.4 = (bf16[8,2176]{1,0:T(8,128)(2,1)S(1)}, bf16[8,2176]{1,0:T(8,128)(2,1)S(1)}, u32[]{:S(2)}, u32[]{:S(2)}) collective-permute-start(bf16[8,2176]{1,0:T(8,128)(2,1)S(1)} %get-tuple-element.22), channel_id=1, source_target_pairs={{0,6},{1,7},{2,4},{3,5},{4,2},{5,3},{6,0},{7,1},{8,13},{9,12},{10,... | collective-permute-start | bytes 104456 | tf_op jit(solution)/shard_map/ppermute | solution.py:286
  25.1 0.5 %collective-permute-start.5 = (bf16[8,2176]{1,0:T(8,128)(2,1)S(1)}, bf16[8,2176]{1,0:T(8,128)(2,1)S(1)}, u32[]{:S(2)}, u32[]{:S(2)}) collective-permute-start(bf16[8,2176]{1,0:T(8,128)(2,1)S(1)} %get-tuple-element.23), channel_id=1, source_target_pairs={{0,4},{1,5},{2,6},{3,7},{4,0},{5,1},{6,2},{7,3},{8,15},{9,14},{10,... | collective-permute-start | bytes 104456 | tf_op jit(solution)/shard_map/ppermute | solution.py:286
  25.6 2.3 %collective-permute-done.4.first.refs_0_ = bf16[8,2176]{1,0:T(8,128)(2,1)S(1)} collective-permute-done((bf16[8,2176]{1,0:T(8,128)(2,1)S(1)}, bf16[8,2176]{1,0:T(8,128)(2,1)S(1)}, u32[]{:S(2)}, u32[]{:S(2)}) %collective-permute-start.4) | collective-permute-done | bytes 34848 | tf_op jit(solution)/shard_map/ppermute | solution.py:286
  27.9 1.2 %collective-permute-done.5.second.refs_1_ = bf16[8,2176]{1,0:T(8,128)(2,1)S(1)} collective-permute-done((bf16[8,2176]{1,0:T(8,128)(2,1)S(1)}, bf16[8,2176]{1,0:T(8,128)(2,1)S(1)}, u32[]{:S(2)}, u32[]{:S(2)}) %collective-permute-start.5) | collective-permute-done | bytes 34848 | tf_op jit(solution)/shard_map/ppermute | solution.py:286
  29.2 0.1 collective-permute-start.6
  29.2 0.0 collective-permute-done.7.refs_1_
  29.3 0.0 collective-permute-done.9.refs_3_
  29.3 0.6 %shard_map.108 = (bf16[1,1,512,768]{3,2,1,0:T(8,128)(2,1)S(1)}, bf16[1,1,768,512]{3,2,1,0:T(8,128)(2,1)S(1)}) custom-call(bf16[32,1280]{1,0:T(8,128)(2,1)S(1)} %get-tuple-element.20.own.refs_0_, bf16[32,1280]{1,0:T(8,128)(2,1)S(1)} %collective-permute-done.7.refs_1_, bf16[32,1792]{1,0:T(8,128)(2,1)S(1)} %collective-permute-done.8.refs_2_, ...), custom_call_target="tpu_custom_call" | custom-call | flops 100663296 | bytes 1572864 | tf_op jit(solution)/shard_map/pallas_call | solution.py:267
  29.9 0.6 %collective-permute-done.6.refs_2_ = bf16[8,2176]{1,0:T(8,128)(2,1)S(1)} collective-permute-done((bf16[8,2176]{1,0:T(8,128)(2,1)S(1)}, bf16[8,2176]{1,0:T(8,128)(2,1)S(1)}, u32[]{:S(2)}, u32[]{:S(2)}) %collective-permute-start.6) | collective-permute-done | bytes 34848 | tf_op jit(solution)/shard_map/ppermute | solution.py:286
  30.4 1.4 %shard_map.109 = (bf16[1,128,2048]{2,1,0:T(8,128)(2,1)}, bf16[1,1,4,4]{3,2,1,0:T(4,128)(2,1)}, bf16[1,1,512,768]{3,2,1,0:T(8,128)(2,1)}, bf16[1,1,768,512]{3,2,1,0:T(8,128)(2,1)}) custom-call(bf16[8,2176]{1,0:T(8,128)(2,1)S(1)} %collective-permute-done.4.first.refs_0_, bf16[8,2176]{1,0:T(8,128)(2,1)S(1)} %collective-permute-done.5.second.refs_1_, ...), custom_call_target="tpu_custom_call" | custom-call | flops 8388608 | bytes 524288 | tf_op jit(solution)/shard_map/pallas_call | solution.py:267
  (3 shorter events, 0.1 us)
Async XLA Ops:
  2.1 1.5 %collective-permute-start = (bf16[8,4224]{1,0:T(8,128)(2,1)S(1)}, bf16[8,4224]{1,0:T(8,128)(2,1)S(1)}, u32[]{:S(2)}, u32[]{:S(2)}) collective-permute-start(bf16[8,4224]{1,0:T(8,128)(2,1)S(1)} %get-tuple-element.17), channel_id=1, source_target_pairs={{0,8},{8,0},{16,24},{24,16},{1,9},{9,1},{17,25},{25,17},{2,10},{10... | collective-permute-start | bytes 202760 | tf_op jit(solution)/shard_map/ppermute | solution.py:286
  3.6 6.3 %copy-start = (bf16[1,1,2048,768]{3,2,1,0:T(8,128)(2,1)S(1)}, bf16[1,1,2048,768]{3,2,1,0:T(8,128)(2,1)}, u32[]{:S(2)}) copy-start(bf16[1,1,2048,768]{3,2,1,0:T(8,128)(2,1)} %up.1) | copy-start | bytes 9437188
  3.6 6.3 %copy-start.1 = (bf16[1,1,768,2048]{3,2,1,0:T(8,128)(2,1)S(1)}, bf16[1,1,768,2048]{3,2,1,0:T(8,128)(2,1)}, u32[]{:S(2)}) copy-start(bf16[1,1,768,2048]{3,2,1,0:T(8,128)(2,1)} %refs_3_.1) | copy-start | bytes 9437188
  3.7 6.3 %collective-permute-start.1 = (bf16[8,4224]{1,0:T(8,128)(2,1)S(1)}, bf16[8,4224]{1,0:T(8,128)(2,1)S(1)}, u32[]{:S(2)}, u32[]{:S(2)}) collective-permute-start(bf16[8,4224]{1,0:T(8,128)(2,1)S(1)} %get-tuple-element.18), channel_id=1, source_target_pairs={{0,2},{1,3},{2,0},{3,1},{8,9},{9,8},{10,11},{11,10},{16,18},{17,19... | collective-permute-start | bytes 202760 | tf_op jit(solution)/shard_map/ppermute | solution.py:286
  7.6 2.3 %collective-permute-start.2 = (bf16[8,4224]{1,0:T(8,128)(2,1)S(1)}, bf16[8,4224]{1,0:T(8,128)(2,1)S(1)}, u32[]{:S(2)}, u32[]{:S(2)}) collective-permute-start(bf16[8,4224]{1,0:T(8,128)(2,1)S(1)} %get-tuple-element.19), channel_id=1, source_target_pairs={{0,0},{1,1},{2,2},{3,3},{8,11},{9,10},{10,9},{11,8},{16,16},{17,17... | collective-permute-start | bytes 202760 | tf_op jit(solution)/shard_map/ppermute | solution.py:286
  11.3 4.8 %collective-permute-start.8 = (bf16[32,1792]{1,0:T(8,128)(2,1)S(1)}, bf16[32,1792]{1,0:T(8,128)(2,1)S(1)}, u32[]{:S(2)}, u32[]{:S(2)}) collective-permute-start(bf16[32,1792]{1,0:T(8,128)(2,1)S(1)} %get-tuple-element.25), channel_id=1, source_target_pairs={{0,16},{8,24},{16,0},{24,8},{1,17},{9,25},{17,1},{25,9},{2,18},{10... | collective-permute-start | bytes 344072 | tf_op jit(solution)/shard_map/ppermute | solution.py:286
  16.1 13.1 %collective-permute-start.9 = (bf16[32,1792]{1,0:T(8,128)(2,1)S(1)}, bf16[32,1792]{1,0:T(8,128)(2,1)S(1)}, u32[]{:S(2)}, u32[]{:S(2)}) collective-permute-start(bf16[32,1792]{1,0:T(8,128)(2,1)S(1)} %collective-permute-done.8.refs_2_), channel_id=1, source_target_pairs={{0,8},{8,0},{16,24},{24,16},{1,9},{9,1},{17,25},{25,17},{2,10},{10... | collective-permute-start | bytes 344072 | tf_op jit(solution)/shard_map/ppermute | solution.py:286
  18.4 10.8 %collective-permute-start.7 = (bf16[32,1280]{1,0:T(8,128)(2,1)S(1)}, bf16[32,1280]{1,0:T(8,128)(2,1)S(1)}, u32[]{:S(2)}, u32[]{:S(2)}) collective-permute-start(bf16[32,1280]{1,0:T(8,128)(2,1)S(1)} %get-tuple-element.24), channel_id=1, source_target_pairs={{0,8},{8,0},{16,24},{24,16},{1,9},{9,1},{17,25},{25,17},{2,10},{10... | collective-permute-start | bytes 245768 | tf_op jit(solution)/shard_map/ppermute | solution.py:286
  18.4 3.6 %collective-permute-start.3 = (bf16[16,128]{1,0:T(8,128)(2,1)S(1)}, bf16[16,128]{1,0:T(8,128)(2,1)S(1)}, u32[]{:S(2)}, u32[]{:S(2)}) collective-permute-start(bf16[16,128]{1,0:T(8,128)(2,1)S(1)} %get-tuple-element.21.tail_own), channel_id=1, source_target_pairs={{0,4},{4,0},{1,5},{5,1},{2,6},{6,2},{3,7},{7,3},{8,12},{12,8},{9,1... | collective-permute-start | bytes 12296 | tf_op jit(solution)/shard_map/ppermute | solution.py:286
  22.0 5.9 %collective-permute-start.4 = (bf16[8,2176]{1,0:T(8,128)(2,1)S(1)}, bf16[8,2176]{1,0:T(8,128)(2,1)S(1)}, u32[]{:S(2)}, u32[]{:S(2)}) collective-permute-start(bf16[8,2176]{1,0:T(8,128)(2,1)S(1)} %get-tuple-element.22), channel_id=1, source_target_pairs={{0,6},{1,7},{2,4},{3,5},{4,2},{5,3},{6,0},{7,1},{8,13},{9,12},{10,... | collective-permute-start | bytes 104456 | tf_op jit(solution)/shard_map/ppermute | solution.py:286
  25.1 4.0 %collective-permute-start.5 = (bf16[8,2176]{1,0:T(8,128)(2,1)S(1)}, bf16[8,2176]{1,0:T(8,128)(2,1)S(1)}, u32[]{:S(2)}, u32[]{:S(2)}) collective-permute-start(bf16[8,2176]{1,0:T(8,128)(2,1)S(1)} %get-tuple-element.23), channel_id=1, source_target_pairs={{0,4},{1,5},{2,6},{3,7},{4,0},{5,1},{6,2},{7,3},{8,15},{9,14},{10,... | collective-permute-start | bytes 104456 | tf_op jit(solution)/shard_map/ppermute | solution.py:286
  29.2 1.3 %collective-permute-start.6 = (bf16[8,2176]{1,0:T(8,128)(2,1)S(1)}, bf16[8,2176]{1,0:T(8,128)(2,1)S(1)}, u32[]{:S(2)}, u32[]{:S(2)}) collective-permute-start(bf16[8,2176]{1,0:T(8,128)(2,1)S(1)} %shard_map.107), channel_id=1, source_target_pairs={{0,8},{8,0},{16,24},{24,16},{1,9},{9,1},{17,25},{25,17},{2,10},{10... | collective-permute-start | bytes 104456 | tf_op jit(solution)/shard_map/ppermute | solution.py:286

commit v4 on v3

--- a/solution.py
+++ b/solution.py
@@ -180,7 +180,8 @@
     blocks = refs[:n_blocks]
     if n_blocks == 1:
         blocks = [blocks[0].at[k] for k in range(blocks[0].shape[0])]
-    grad_up, grad_down = refs[n_blocks:]
+    up_far, grad_down, grad_up, sem = refs[n_blocks:]
+    up_out = pltpu.make_async_copy(grad_up, up_far, sem.at[0])
 
     def first_of(value):
         row = lax.broadcasted_iota(jnp.int32, value.shape, 0)
@@ -201,15 +202,23 @@
     grad_up[0, 0] = lax.dot_general(
         sides, act_grad, (((0,), (0,)), ((), ())), preferred_element_type=F32
     ).astype(BF16)
+    up_out.start()
     scaled = jnp.where(first_of(sides), jnp.zeros_like(sides), sides)
     grad_down[0, 0] = lax.dot_general(
         both, scaled, (((0,), (0,)), ((), ())), preferred_element_type=F32
     ).astype(BF16)
+    up_out.wait()
+
+
+def flush_kernel(down, _, down_far, sem):
+    copy = pltpu.make_async_copy(down, down_far, sem.at[0])
+    copy.start()
+    copy.wait()
 
 
 def combine_kernel(capacity, sections, n_blocks, *refs):
     blocks = refs[:n_blocks]
-    up_near, down_near, prev_far, gate_far, up_far, down_far, prev, gate, sems = refs[n_blocks:]
+    prev_far, gate_far, prev, gate, sems = refs[n_blocks:]
     tokens, width = prev.shape[1:]
     experts = gate.shape[2]
     paired = in_pairs(experts, lax.axis_size("dp"))
@@ -217,10 +226,8 @@
     rows = capacity * experts
     spans = [pl.ds(k * half, half) for k in range(2)]
     pairs = [(prev.at[:, :, span], prev_far.at[:, :, span]) for span in spans]
-    pairs += [(gate, gate_far), (up_near, up_far), (down_near, down_far)]
+    pairs.append((gate, gate_far))
     copies = [pltpu.make_async_copy(a, b, sems.at[k]) for k, (a, b) in enumerate(pairs)]
-    copies[3].start()
-    copies[4].start()
     if paired:
         first, second, came = [block[...].astype(F32) for block in blocks]
         mine = jnp.where(upper_rows(first), first, turned(second))
@@ -255,20 +262,21 @@
         copy.wait()
 
 
-def call(kernel, out_shape, args, flops, n_bytes, scratch=(), far=(), far_out=False):
+def call(kernel, out_shape, args, flops, n_bytes, scratch=(), far=(), far_out=()):
     near_spec = pl.BlockSpec(memory_space=pltpu.VMEM)
     far_spec = pl.BlockSpec(memory_space=pl.ANY)
     args = [
         pltpu.with_memory_space_constraint(a, pltpu.HBM if k in far else pltpu.VMEM)
         for k, a in enumerate(args)
     ]
-    if not far_out:
-        out_shape = [pltpu.VMEM(s.shape, s.dtype) for s in out_shape]
+    out_shape = [
+        s if k in far_out else pltpu.VMEM(s.shape, s.dtype) for k, s in enumerate(out_shape)
+    ]
     return pl.pallas_call(
         kernel,
         out_shape=out_shape,
         in_specs=[far_spec if k in far else near_spec for k in range(len(args))],
-        out_specs=[far_spec if far_out else near_spec] * len(out_shape),
+        out_specs=[far_spec if k in far_out else near_spec for k in range(len(out_shape))],
         scratch_shapes=list(scratch),
         compiler_params=pltpu.CompilerParams(vmem_limit_bytes=KERNEL_VMEM),
         cost_estimate=pl.CostEstimate(flops=flops, bytes_accessed=n_bytes, transcendentals=0),
@@ -406,25 +414,36 @@
         jax.ShapeDtypeStruct((1, 1, part, hidden_width), BF16),
         jax.ShapeDtypeStruct((1, 1, hidden_width, part), BF16),
     ]
-    near_grads = call(
+    grad_up, near_down = call(
         functools.partial(weight_kernel, rows, len(joined)),
         weight_grads,
         tuple(joined),
         4 * replicas * rows * part * hidden_width,
         4 * part * hidden_width,
+        [pltpu.VMEM(weight_grads[0].shape, BF16), pltpu.SemaphoreType.DMA((1,))],
+        far_out=(0,),
+    )
+    (grad_down,) = call(
+        flush_kernel,
+        weight_grads[1:],
+        (near_down, returned[0]),
+        0,
+        8 * part * hidden_width,
+        [pltpu.SemaphoreType.DMA((1,))],
+        far_out=(0,),
     )
     token_grads = [
         jax.ShapeDtypeStruct((1, tokens, width), BF16),
         jax.ShapeDtypeStruct((1, 1, experts, capacity), BF16),
     ]
-    grad_prev, grad_gate, grad_up, grad_down = call(
+    grad_prev, grad_gate = call(
         functools.partial(combine_kernel, capacity, sections, len(returned)),
-        token_grads + weight_grads,
-        (*returned, *near_grads),
+        token_grads,
+        tuple(returned),
         2 * rows * tokens * width,
         2 * tokens * width,
-        [pltpu.VMEM(s.shape, s.dtype) for s in token_grads] + [pltpu.SemaphoreType.DMA((5,))],
-        far_out=True,
+        [pltpu.VMEM(s.shape, s.dtype) for s in token_grads] + [pltpu.SemaphoreType.DMA((3,))],
+        far_out=(0, 1),
     )
     return grad_prev, grad_gate, grad_up, grad_down
 

time: 32 us -> 34 us (1.062)
  Pallas kernels: 5.84 us -> 7.21 us
  waiting for transfers between devices: 10.6 us -> 11.2 us
    pallas_call x8 -> x9, Pallas kernels: 5.84 us -> 7.21 us  [call(): pl.pallas_call(kernel, out_shape=out_shape, in_specs=[far_spec if k in fa...]
    ppermute x10, waiting for transfers between devices: 10.6 us -> 11.2 us  [permuted(): return lax.ppermute(block, axes if len(axes) > 1 else axes[0], pairs)]
  transfers between devices with their start and end apart: 10 -> 10, of which waited for: 7 -> 7; matrix products, arithmetic and copies ran while one was open for 0% -> 0% of each run, Pallas kernels for 5% -> 6%
where the time goes in v4:
time: 34 us; the launch traced here: 33.8 us
  starting transfers between devices  14.6 us (43%)
  waiting for transfers between devices  11.2 us (33%)
  Pallas kernels  7.21 us (21%)
  between operations  0.71 us (2%)
    ppermute x10, starting transfers between devices, permuted(): return lax.ppermute(block, axes if len(axes) > 1 else axes[0], pairs)  14.6 us
    ppermute x10, waiting for transfers between devices, permuted(): return lax.ppermute(block, axes if len(axes) > 1 else axes[0], pairs)  11.2 us
    pallas_call x9, Pallas kernels, call(): pl.pallas_call(kernel, out_shape=out_shape, in_specs=[far_spec if k in fa...  7.21 us
  transfers between devices with their start and end apart: 10, of which 7 were waited for; matrix products, arithmetic and copies ran while one was open for 0% of the time, Pallas kernels for 6%

profile of v4, /device:TPU:0, one launch (start us, length us, event | category | flops | bytes accessed | tf_op | source)
XLA Modules:
  0.0 33.8 jit_solution(11199845469584565727)
XLA Ops:
  0.6 1.5 %shard_map.102 = (bf16[8,4224]{1,0:T(8,128)(2,1)S(1)}, bf16[8,4224]{1,0:T(8,128)(2,1)S(1)}) custom-call(bf16[1,128,2048]{2,1,0:T(8,128)(2,1)} %acts_far.1, bf16[1,128,2048]{2,1,0:T(8,128)(2,1)} %grads_far.1, s32[1,1,4,4]{3,2,1,0:T(4,128)} %ids_far.1, s32[1,1,4]{2,1,0:T(1,128)} %counts_far.1, bf16[1,1,4,4]{3,2,1,0:T(4,128)(2,1)} %probs_far.1), custom_call_target="tpu_custom_call" | custom-call | flops 16777216 | bytes 1048576 | tf_op jit(solution)/shard_map/pallas_call | solution.py:275
  2.1 0.6 %collective-permute-start = (bf16[8,4224]{1,0:T(8,128)(2,1)S(1)}, bf16[8,4224]{1,0:T(8,128)(2,1)S(1)}, u32[]{:S(2)}, u32[]{:S(2)}) collective-permute-start(bf16[8,4224]{1,0:T(8,128)(2,1)S(1)} %get-tuple-element.19), channel_id=1, source_target_pairs={{0,8},{8,0},{16,24},{24,16},{1,9},{9,1},{17,25},{25,17},{2,10},{10... | collective-permute-start | bytes 202760 | tf_op jit(solution)/shard_map/ppermute | solution.py:294
  2.7 0.9 %collective-permute-done.came = bf16[8,4224]{1,0:T(8,128)(2,1)S(1)} collective-permute-done((bf16[8,4224]{1,0:T(8,128)(2,1)S(1)}, bf16[8,4224]{1,0:T(8,128)(2,1)S(1)}, u32[]{:S(2)}, u32[]{:S(2)}) %collective-permute-start) | collective-permute-done | bytes 67616 | tf_op jit(solution)/shard_map/ppermute | solution.py:294
  3.6 0.0 copy-start
  3.6 0.0 copy-start.1
  3.7 4.0 %collective-permute-start.1 = (bf16[8,4224]{1,0:T(8,128)(2,1)S(1)}, bf16[8,4224]{1,0:T(8,128)(2,1)S(1)}, u32[]{:S(2)}, u32[]{:S(2)}) collective-permute-start(bf16[8,4224]{1,0:T(8,128)(2,1)S(1)} %get-tuple-element.20), channel_id=1, source_target_pairs={{0,2},{1,3},{2,0},{3,1},{8,9},{9,8},{10,11},{11,10},{16,18},{17,19... | collective-permute-start | bytes 202760 | tf_op jit(solution)/shard_map/ppermute | solution.py:294
  7.6 0.7 %collective-permute-start.2 = (bf16[8,4224]{1,0:T(8,128)(2,1)S(1)}, bf16[8,4224]{1,0:T(8,128)(2,1)S(1)}, u32[]{:S(2)}, u32[]{:S(2)}) collective-permute-start(bf16[8,4224]{1,0:T(8,128)(2,1)S(1)} %get-tuple-element.21), channel_id=1, source_target_pairs={{0,0},{1,1},{2,2},{3,3},{8,11},{9,10},{10,9},{11,8},{16,16},{17,17... | collective-permute-start | bytes 202760 | tf_op jit(solution)/shard_map/ppermute | solution.py:294
  8.3 1.6 %collective-permute-done.1.refs_0_ = bf16[8,4224]{1,0:T(8,128)(2,1)S(1)} collective-permute-done((bf16[8,4224]{1,0:T(8,128)(2,1)S(1)}, bf16[8,4224]{1,0:T(8,128)(2,1)S(1)}, u32[]{:S(2)}, u32[]{:S(2)}) %collective-permute-start.1) | collective-permute-done | bytes 67616 | tf_op jit(solution)/shard_map/ppermute | solution.py:294
  9.9 0.0 collective-permute-done.2.refs_1_
  9.9 0.0 copy-done
  9.9 0.0 copy-done.1
  9.9 1.4 %shard_map.104 = (bf16[32,1280]{1,0:T(8,128)(2,1)S(1)}, bf16[32,1280]{1,0:T(8,128)(2,1)S(1)}, bf16[32,1792]{1,0:T(8,128)(2,1)S(1)}, bf16[16,128]{1,0:T(8,128)(2,1)S(1)}) custom-call(bf16[8,4224]{1,0:T(8,128)(2,1)S(1)} %collective-permute-done.1.refs_0_, bf16[8,4224]{1,0:T(8,128)(2,1)S(1)} %collective-permute-done.2.refs_1_, ...), custom_call_target="tpu_custom_call" | custom-call | flops 100663296 | bytes 6291456 | tf_op jit(solution)/shard_map/pallas_call | solution.py:275
  11.3 1.9 %collective-permute-start.8 = (bf16[32,1792]{1,0:T(8,128)(2,1)S(1)}, bf16[32,1792]{1,0:T(8,128)(2,1)S(1)}, u32[]{:S(2)}, u32[]{:S(2)}) collective-permute-start(bf16[32,1792]{1,0:T(8,128)(2,1)S(1)} %get-tuple-element.29), channel_id=1, source_target_pairs={{0,16},{8,24},{16,0},{24,8},{1,17},{9,25},{17,1},{25,9},{2,18},{10... | collective-permute-start | bytes 344072 | tf_op jit(solution)/shard_map/ppermute | solution.py:294
  13.2 2.9 %collective-permute-done.8.refs_2_ = bf16[32,1792]{1,0:T(8,128)(2,1)S(1)} collective-permute-done((bf16[32,1792]{1,0:T(8,128)(2,1)S(1)}, bf16[32,1792]{1,0:T(8,128)(2,1)S(1)}, u32[]{:S(2)}, u32[]{:S(2)}) %collective-permute-start.8) | collective-permute-done | bytes 114720 | tf_op jit(solution)/shard_map/ppermute | solution.py:294
  16.1 2.3 %collective-permute-start.9 = (bf16[32,1792]{1,0:T(8,128)(2,1)S(1)}, bf16[32,1792]{1,0:T(8,128)(2,1)S(1)}, u32[]{:S(2)}, u32[]{:S(2)}) collective-permute-start(bf16[32,1792]{1,0:T(8,128)(2,1)S(1)} %collective-permute-done.8.refs_2_), channel_id=1, source_target_pairs={{0,8},{8,0},{16,24},{24,16},{1,9},{9,1},{17,25},{25,17},{2,10},{10... | collective-permute-start | bytes 344072 | tf_op jit(solution)/shard_map/ppermute | solution.py:294
  18.4 0.0 collective-permute-start.7
  18.4 1.6 %collective-permute-start.3 = (bf16[16,128]{1,0:T(8,128)(2,1)S(1)}, bf16[16,128]{1,0:T(8,128)(2,1)S(1)}, u32[]{:S(2)}, u32[]{:S(2)}) collective-permute-start(bf16[16,128]{1,0:T(8,128)(2,1)S(1)} %get-tuple-element.23.tail_own), channel_id=1, source_target_pairs={{0,4},{4,0},{1,5},{5,1},{2,6},{6,2},{3,7},{7,3},{8,12},{12,8},{9,1... | collective-permute-start | bytes 12296 | tf_op jit(solution)/shard_map/ppermute | solution.py:294
  20.0 0.9 %shard_map.105.body = bf16[16,2048]{1,0:T(8,128)(2,1)S(1)} custom-call(bf16[32,1280]{1,0:T(8,128)(2,1)S(1)} %get-tuple-element.22.own.refs_0_, bf16[1,1,2048,768]{3,2,1,0:T(8,128)(2,1)S(1)} %copy-done), custom_call_target="tpu_custom_call" | custom-call | flops 50331648 | bytes 3145728 | tf_op jit(solution)/shard_map/pallas_call | solution.py:275
  20.9 1.1 %collective-permute-done.3.tail_other = bf16[16,128]{1,0:T(8,128)(2,1)S(1)} collective-permute-done((bf16[16,128]{1,0:T(8,128)(2,1)S(1)}, bf16[16,128]{1,0:T(8,128)(2,1)S(1)}, u32[]{:S(2)}, u32[]{:S(2)}) %collective-permute-start.3) | collective-permute-done | bytes 4128 | tf_op jit(solution)/shard_map/ppermute | solution.py:294
  22.0 3.1 %collective-permute-start.4 = (bf16[8,2176]{1,0:T(8,128)(2,1)S(1)}, bf16[8,2176]{1,0:T(8,128)(2,1)S(1)}, u32[]{:S(2)}, u32[]{:S(2)}) collective-permute-start(bf16[8,2176]{1,0:T(8,128)(2,1)S(1)} %get-tuple-element.24), channel_id=1, source_target_pairs={{0,6},{1,7},{2,4},{3,5},{4,2},{5,3},{6,0},{7,1},{8,13},{9,12},{10,... | collective-permute-start | bytes 104456 | tf_op jit(solution)/shard_map/ppermute | solution.py:294
  25.1 0.5 %collective-permute-start.5 = (bf16[8,2176]{1,0:T(8,128)(2,1)S(1)}, bf16[8,2176]{1,0:T(8,128)(2,1)S(1)}, u32[]{:S(2)}, u32[]{:S(2)}) collective-permute-start(bf16[8,2176]{1,0:T(8,128)(2,1)S(1)} %get-tuple-element.25), channel_id=1, source_target_pairs={{0,4},{1,5},{2,6},{3,7},{4,0},{5,1},{6,2},{7,3},{8,15},{9,14},{10,... | collective-permute-start | bytes 104456 | tf_op jit(solution)/shard_map/ppermute | solution.py:294
  25.6 2.3 %collective-permute-done.4.first.refs_0_._ = bf16[8,2176]{1,0:T(8,128)(2,1)S(1)} collective-permute-done((bf16[8,2176]{1,0:T(8,128)(2,1)S(1)}, bf16[8,2176]{1,0:T(8,128)(2,1)S(1)}, u32[]{:S(2)}, u32[]{:S(2)}) %collective-permute-start.4) | collective-permute-done | bytes 34848 | tf_op jit(solution)/shard_map/ppermute | solution.py:294
  27.9 1.2 %collective-permute-done.5.second.refs_1_ = bf16[8,2176]{1,0:T(8,128)(2,1)S(1)} collective-permute-done((bf16[8,2176]{1,0:T(8,128)(2,1)S(1)}, bf16[8,2176]{1,0:T(8,128)(2,1)S(1)}, u32[]{:S(2)}, u32[]{:S(2)}) %collective-permute-start.5) | collective-permute-done | bytes 34848 | tf_op jit(solution)/shard_map/ppermute | solution.py:294
  29.2 0.1 collective-permute-start.6
  29.2 1.2 %collective-permute-done.6.refs_2_ = bf16[8,2176]{1,0:T(8,128)(2,1)S(1)} collective-permute-done((bf16[8,2176]{1,0:T(8,128)(2,1)S(1)}, bf16[8,2176]{1,0:T(8,128)(2,1)S(1)}, u32[]{:S(2)}, u32[]{:S(2)}) %collective-permute-start.6) | collective-permute-done | bytes 34848 | tf_op jit(solution)/shard_map/ppermute | solution.py:294
  30.4 1.1 %shard_map.108 = (bf16[1,128,2048]{2,1,0:T(8,128)(2,1)}, bf16[1,1,4,4]{3,2,1,0:T(4,128)(2,1)}) custom-call(bf16[8,2176]{1,0:T(8,128)(2,1)S(1)} %collective-permute-done.4.first.refs_0_._, bf16[8,2176]{1,0:T(8,128)(2,1)S(1)} %collective-permute-done.5.second.refs_1_, bf16[8,2176]{1,0:T(8,128)(2,1)S(1)} %collective-permute-done.6.refs_2_), custom_call_target="tpu_custom_call" | custom-call | flops 8388608 | bytes 524288 | tf_op jit(solution)/shard_map/pallas_call | solution.py:275
  31.6 0.0 collective-permute-done.7.refs_1_
  31.6 0.0 collective-permute-done.9.refs_3_
  31.6 1.3 %shard_map.109 = (bf16[1,1,512,768]{3,2,1,0:T(8,128)(2,1)}, bf16[1,1,768,512]{3,2,1,0:T(8,128)(2,1)S(1)}) custom-call(bf16[32,1280]{1,0:T(8,128)(2,1)S(1)} %get-tuple-element.22.own.refs_0_, bf16[32,1280]{1,0:T(8,128)(2,1)S(1)} %collective-permute-done.7.refs_1_, bf16[32,1792]{1,0:T(8,128)(2,1)S(1)} %collective-permute-done.8.refs_2_, ...), custom_call_target="tpu_custom_call" | custom-call | flops 100663296 | bytes 1572864 | tf_op jit(solution)/shard_map/pallas_call | solution.py:275
  32.9 0.9 %shard_map.110 = bf16[1,1,768,512]{3,2,1,0:T(8,128)(2,1)} custom-call(bf16[1,1,768,512]{3,2,1,0:T(8,128)(2,1)S(1)} %get-tuple-element.31.down, bf16[8,2176]{1,0:T(8,128)(2,1)S(1)} %collective-permute-done.4.first.refs_0_._), custom_call_target="tpu_custom_call" | custom-call | bytes 3145728 | tf_op jit(solution)/shard_map/pallas_call | solution.py:275
  (3 shorter events, 0.1 us)
Async XLA Ops:
  2.1 1.5 %collective-permute-start = (bf16[8,4224]{1,0:T(8,128)(2,1)S(1)}, bf16[8,4224]{1,0:T(8,128)(2,1)S(1)}, u32[]{:S(2)}, u32[]{:S(2)}) collective-permute-start(bf16[8,4224]{1,0:T(8,128)(2,1)S(1)} %get-tuple-element.19), channel_id=1, source_target_pairs={{0,8},{8,0},{16,24},{24,16},{1,9},{9,1},{17,25},{25,17},{2,10},{10... | collective-permute-start | bytes 202760 | tf_op jit(solution)/shard_map/ppermute | solution.py:294
  3.6 6.3 %copy-start = (bf16[1,1,2048,768]{3,2,1,0:T(8,128)(2,1)S(1)}, bf16[1,1,2048,768]{3,2,1,0:T(8,128)(2,1)}, u32[]{:S(2)}) copy-start(bf16[1,1,2048,768]{3,2,1,0:T(8,128)(2,1)} %up.1) | copy-start | bytes 9437188
  3.6 6.3 %copy-start.1 = (bf16[1,1,768,2048]{3,2,1,0:T(8,128)(2,1)S(1)}, bf16[1,1,768,2048]{3,2,1,0:T(8,128)(2,1)}, u32[]{:S(2)}) copy-start(bf16[1,1,768,2048]{3,2,1,0:T(8,128)(2,1)} %refs_3_.1) | copy-start | bytes 9437188
  3.7 6.3 %collective-permute-start.1 = (bf16[8,4224]{1,0:T(8,128)(2,1)S(1)}, bf16[8,4224]{1,0:T(8,128)(2,1)S(1)}, u32[]{:S(2)}, u32[]{:S(2)}) collective-permute-start(bf16[8,4224]{1,0:T(8,128)(2,1)S(1)} %get-tuple-element.20), channel_id=1, source_target_pairs={{0,2},{1,3},{2,0},{3,1},{8,9},{9,8},{10,11},{11,10},{16,18},{17,19... | collective-permute-start | bytes 202760 | tf_op jit(solution)/shard_map/ppermute | solution.py:294
  7.6 2.3 %collective-permute-start.2 = (bf16[8,4224]{1,0:T(8,128)(2,1)S(1)}, bf16[8,4224]{1,0:T(8,128)(2,1)S(1)}, u32[]{:S(2)}, u32[]{:S(2)}) collective-permute-start(bf16[8,4224]{1,0:T(8,128)(2,1)S(1)} %get-tuple-element.21), channel_id=1, source_target_pairs={{0,0},{1,1},{2,2},{3,3},{8,11},{9,10},{10,9},{11,8},{16,16},{17,17... | collective-permute-start | bytes 202760 | tf_op jit(solution)/shard_map/ppermute | solution.py:294
  11.3 4.8 %collective-permute-start.8 = (bf16[32,1792]{1,0:T(8,128)(2,1)S(1)}, bf16[32,1792]{1,0:T(8,128)(2,1)S(1)}, u32[]{:S(2)}, u32[]{:S(2)}) collective-permute-start(bf16[32,1792]{1,0:T(8,128)(2,1)S(1)} %get-tuple-element.29), channel_id=1, source_target_pairs={{0,16},{8,24},{16,0},{24,8},{1,17},{9,25},{17,1},{25,9},{2,18},{10... | collective-permute-start | bytes 344072 | tf_op jit(solution)/shard_map/ppermute | solution.py:294
  16.1 15.4 %collective-permute-start.9 = (bf16[32,1792]{1,0:T(8,128)(2,1)S(1)}, bf16[32,1792]{1,0:T(8,128)(2,1)S(1)}, u32[]{:S(2)}, u32[]{:S(2)}) collective-permute-start(bf16[32,1792]{1,0:T(8,128)(2,1)S(1)} %collective-permute-done.8.refs_2_), channel_id=1, source_target_pairs={{0,8},{8,0},{16,24},{24,16},{1,9},{9,1},{17,25},{25,17},{2,10},{10... | collective-permute-start | bytes 344072 | tf_op jit(solution)/shard_map/ppermute | solution.py:294
  18.4 13.2 %collective-permute-start.7 = (bf16[32,1280]{1,0:T(8,128)(2,1)S(1)}, bf16[32,1280]{1,0:T(8,128)(2,1)S(1)}, u32[]{:S(2)}, u32[]{:S(2)}) collective-permute-start(bf16[32,1280]{1,0:T(8,128)(2,1)S(1)} %get-tuple-element.28), channel_id=1, source_target_pairs={{0,8},{8,0},{16,24},{24,16},{1,9},{9,1},{17,25},{25,17},{2,10},{10... | collective-permute-start | bytes 245768 | tf_op jit(solution)/shard_map/ppermute | solution.py:294
  18.4 3.6 %collective-permute-start.3 = (bf16[16,128]{1,0:T(8,128)(2,1)S(1)}, bf16[16,128]{1,0:T(8,128)(2,1)S(1)}, u32[]{:S(2)}, u32[]{:S(2)}) collective-permute-start(bf16[16,128]{1,0:T(8,128)(2,1)S(1)} %get-tuple-element.23.tail_own), channel_id=1, source_target_pairs={{0,4},{4,0},{1,5},{5,1},{2,6},{6,2},{3,7},{7,3},{8,12},{12,8},{9,1... | collective-permute-start | bytes 12296 | tf_op jit(solution)/shard_map/ppermute | solution.py:294
  22.0 5.9 %collective-permute-start.4 = (bf16[8,2176]{1,0:T(8,128)(2,1)S(1)}, bf16[8,2176]{1,0:T(8,128)(2,1)S(1)}, u32[]{:S(2)}, u32[]{:S(2)}) collective-permute-start(bf16[8,2176]{1,0:T(8,128)(2,1)S(1)} %get-tuple-element.24), channel_id=1, source_target_pairs={{0,6},{1,7},{2,4},{3,5},{4,2},{5,3},{6,0},{7,1},{8,13},{9,12},{10,... | collective-permute-start | bytes 104456 | tf_op jit(solution)/shard_map/ppermute | solution.py:294
  25.1 4.0 %collective-permute-start.5 = (bf16[8,2176]{1,0:T(8,128)(2,1)S(1)}, bf16[8,2176]{1,0:T(8,128)(2,1)S(1)}, u32[]{:S(2)}, u32[]{:S(2)}) collective-permute-start(bf16[8,2176]{1,0:T(8,128)(2,1)S(1)} %get-tuple-element.25), channel_id=1, source_target_pairs={{0,4},{1,5},{2,6},{3,7},{4,0},{5,1},{6,2},{7,3},{8,15},{9,14},{10,... | collective-permute-start | bytes 104456 | tf_op jit(solution)/shard_map/ppermute | solution.py:294
  29.2 1.3 %collective-permute-start.6 = (bf16[8,2176]{1,0:T(8,128)(2,1)S(1)}, bf16[8,2176]{1,0:T(8,128)(2,1)S(1)}, u32[]{:S(2)}, u32[]{:S(2)}) collective-permute-start(bf16[8,2176]{1,0:T(8,128)(2,1)S(1)} %shard_map.107), channel_id=1, source_target_pairs={{0,8},{8,0},{16,24},{24,16},{1,9},{9,1},{17,25},{25,17},{2,10},{10... | collective-permute-start | bytes 104456 | tf_op jit(solution)/shard_map/ppermute | solution.py:294
